TPU v7x, 256 devices: a whole 4x4x8 slice. The times are simulated.
256 devices in a mesh: seq: 128 (over y_lo, x, z, core), req: 2 (over y_hi).
Axes of the slice: x: 4, y: 4 (y_hi: 2, y_lo: 2; y = y_hi * 2 + y_lo), z: 8, core: 2. Of those that a mesh axis runs over, the one named last changes fastest.
Arguments:
- tokens: bfloat16 [16384, 2048], P('seq'), may hold values from -6 to 6
- norm_gain: float32 [2048], replicated, may hold values from 0.5 to 1.5
- w_query: bfloat16 [2048, 1024], P(None, 'req'), as said below
- key_projection: bfloat16 [2048, 512], P(None, 'req')
- value_projection: bfloat16 [2048, 512], P(None, 'req'), may hold values from -0.125 to 0.125
- w_out: bfloat16 [1024, 2048], P('req'), may hold values from -0.1875 to 0.1875
- lengths: int32 [4], replicated, may hold values from 1 to 10922, 16384 in all
- block_split: int32 [128], replicated, may hold values from 0 to 127, each once
- page_slot: int32 [512], replicated, may hold values from 0 to 1023, as said below
Outputs:
- hidden: bfloat16 [16384, 2048], P(('seq', 'req'))
- key_value_cache: bfloat16 [1024, 2, 32, 512], P('seq', None, None, 'req')
Inputs may be any that keep to these rules, and one draw needn't show every extreme that they name: block_split is a permutation; index i of seq holds block block_split[i] and its mirror. `page_slot`: distinct slots; slot s lies on index s // 8 of seq. `w_query`: a projection scaled like 2 / sqrt(2048).
All inputs are finite; a program needn't handle non-finite values.
Results may differ from a plain program's by a relative error of at most 0.014.
The roundings to bfloat16 on the way count: a program that leaves them out, or rounds other values in their place, can miss the bound.
Values may be sent and summed in bfloat16 or wider, within the bound.
A program may use at most 128 MiB of HBM per device.

v0:
```python
import math

import jax
import jax.numpy as jnp
from jax import lax
from jax.sharding import PartitionSpec as P

HEAD_SIZE = 128
PAGE_TOKENS = 32


theta_base = 1000000.0
norm_eps = 1e-05
far_below = -1e30


def rotary_rows(heads, offset_list):
    half_width = heads.shape[-1] // 2
    exponent = jnp.arange(half_width, dtype=jnp.float32) * (2.0 / heads.shape[-1])
    inv_freq = jnp.power(theta_base, -exponent)
    angle = offset_list.astype(jnp.float32)[:, None] * inv_freq[None, :]
    cosine = jnp.concatenate([jnp.cos(angle), jnp.cos(angle)], -1)[:, None, :]
    sine = jnp.concatenate([jnp.sin(angle), jnp.sin(angle)], -1)[:, None, :]
    rolled = jnp.concatenate([-heads[..., half_width:], heads[..., :half_width]], -1)
    return heads * cosine + rolled * sine


def slot_positions(block_split, lengths, total_rows, shard_rows):
    row_ids = jnp.arange(total_rows, dtype=jnp.int32)
    half_rows = shard_rows // 2
    cycle_size = block_split.shape[0]
    owner_dev = row_ids // shard_rows
    device_ids = jnp.arange(cycle_size, dtype=jnp.int32)
    first_block = jnp.sum(
        jnp.where(owner_dev[:, None] == device_ids[None, :], block_split[None, :], 0), 1
    )
    block_ids = jnp.where(
        row_ids % shard_rows < half_rows, first_block, 2 * cycle_size - 1 - first_block
    )
    position = block_ids * half_rows + row_ids % half_rows
    request_ends = jnp.cumsum(lengths)
    request_begins = request_ends - lengths
    request = jnp.sum((position[:, None] >= request_ends[None, :]).astype(jnp.int32), 1)
    prompt_ids = jnp.arange(lengths.shape[0], dtype=jnp.int32)
    begins = jnp.sum(
        jnp.where(request[:, None] == prompt_ids[None, :], request_begins[None, :], 0), 1
    )
    return (position, request, position - begins)


def on_device(
    tokens,
    norm_gain,
    w_query,
    key_projection,
    value_projection,
    w_out,
    lengths,
    block_split,
    page_slot,
):
    shard_rows = tokens.shape[0]
    half_rows = shard_rows // 2
    cycle_size = lax.axis_size("seq")
    device = lax.axis_index("seq")
    first_row = device * shard_rows
    position, request, offset_list = slot_positions(
        block_split, lengths, shard_rows * cycle_size, shard_rows
    )
    q_pos = lax.dynamic_slice_in_dim(position, first_row, shard_rows, 0)
    q_req = lax.dynamic_slice_in_dim(request, first_row, shard_rows, 0)
    q_off = lax.dynamic_slice_in_dim(offset_list, first_row, shard_rows, 0)
    cache_rows = 2 * shard_rows
    slot_count = cache_rows // PAGE_TOKENS
    slot_ids = page_slot[position // PAGE_TOKENS]
    holder = slot_ids // slot_count
    target_rows = jnp.where(
        holder == device, slot_ids % slot_count * PAGE_TOKENS + position % PAGE_TOKENS, -1
    )
    heads_local = w_query.shape[1] // HEAD_SIZE
    kv_local = key_projection.shape[1] // HEAD_SIZE
    group_width = heads_local // kv_local
    scale_factor = 1.0 / math.sqrt(HEAD_SIZE)
    widened = tokens.astype(jnp.float32)
    normalized_input = (
        widened * lax.rsqrt(jnp.mean(widened * widened, -1, keepdims=True) + norm_eps) * norm_gain
    ).astype(jnp.bfloat16)
    queries = rotary_rows(
        jnp.dot(normalized_input, w_query, preferred_element_type=jnp.float32).reshape(
            shard_rows, heads_local, HEAD_SIZE
        ),
        q_off,
    )
    queries = queries.astype(jnp.bfloat16).reshape(shard_rows, kv_local, group_width, HEAD_SIZE)
    key_matrix_rows = rotary_rows(
        jnp.dot(normalized_input, key_projection, preferred_element_type=jnp.float32).reshape(
            shard_rows, kv_local, HEAD_SIZE
        ),
        q_off,
    )
    key_matrix_rows = key_matrix_rows.astype(jnp.bfloat16).reshape(shard_rows, kv_local * HEAD_SIZE)
    value_matrix_rows = jnp.dot(
        normalized_input, value_projection, preferred_element_type=jnp.float32
    ).astype(jnp.bfloat16)

    def attend(moments, key_block, value_block, visible):
        run_max, run_sum, run_acc = moments
        width = key_block.shape[0]
        key_heads = key_block.reshape(width, kv_local, HEAD_SIZE)
        value_heads = value_block.reshape(width, kv_local, HEAD_SIZE)
        scores = (
            jnp.einsum("qhgd,khd->hgqk", queries, key_heads, preferred_element_type=jnp.float32)
            * scale_factor
        )
        masked = jnp.where(visible[None, None], scores, far_below)
        new_max = jnp.maximum(run_max, jnp.max(masked, -1))
        weights = jnp.where(visible[None, None], jnp.exp(masked - new_max[..., None]), 0.0)
        factor = jnp.exp(run_max - new_max)
        new_sum = run_sum * factor + jnp.sum(weights, -1)
        added = jnp.einsum(
            "hgqk,khd->hgqd",
            weights.astype(jnp.bfloat16),
            value_heads,
            preferred_element_type=jnp.float32,
        )
        return (new_max, new_sum, run_acc * factor[..., None] + added)

    def store(parts, key_block, value_block, key_target):
        cache_grid = jnp.arange(cache_rows, dtype=jnp.int32)
        placer = (cache_grid[:, None] == key_target[None, :]).astype(jnp.bfloat16)
        return (
            parts[0] + jnp.dot(placer, key_block, preferred_element_type=jnp.float32),
            parts[1] + jnp.dot(placer, value_block, preferred_element_type=jnp.float32),
        )

    start_max = jnp.full((kv_local, group_width, shard_rows), far_below, jnp.float32)
    start_sum = jnp.zeros((kv_local, group_width, shard_rows), jnp.float32)
    start_acc = jnp.zeros((kv_local, group_width, shard_rows, HEAD_SIZE), jnp.float32)
    start_keys = jnp.zeros((cache_rows, kv_local * HEAD_SIZE), jnp.float32)
    start_values = jnp.zeros((cache_rows, kv_local * HEAD_SIZE), jnp.float32)
    state = (start_max, start_sum, start_acc, start_keys, start_values)
    absorb_state = state
    key_piece = lax.all_gather(key_matrix_rows, "seq", axis=0, tiled=True)
    value_piece = lax.all_gather(value_matrix_rows, "seq", axis=0, tiled=True)
    length = key_piece.shape[0]
    sub_width = math.gcd(length, 1024)

    def sub_step(carried, sub_index):
        offset = sub_index * sub_width
        key_block = lax.dynamic_slice_in_dim(key_piece, offset, sub_width, 0)
        value_block = lax.dynamic_slice_in_dim(value_piece, offset, sub_width, 0)
        key_pos = lax.dynamic_slice_in_dim(position, offset, sub_width, 0)
        key_req = lax.dynamic_slice_in_dim(request, offset, sub_width, 0)
        key_target = lax.dynamic_slice_in_dim(target_rows, offset, sub_width, 0)
        visible = (key_req[None, :] == q_req[:, None]) & (key_pos[None, :] <= q_pos[:, None])
        moments = carried[:3]
        cache_parts = carried[3:]
        moments = attend(moments, key_block, value_block, visible)
        cache_parts = lax.cond(
            jnp.any(key_target >= 0),
            store,
            lambda parts, key_block, value_block, key_target: parts,
            cache_parts,
            key_block,
            value_block,
            key_target,
        )
        return (moments + cache_parts, None)

    absorb_state, _ = lax.scan(
        sub_step, absorb_state, jnp.arange(length // sub_width, dtype=jnp.int32)
    )
    state = absorb_state
    run_max, run_sum, run_acc, cache_keys, cache_values = state
    normalised = run_acc / run_sum[..., None]
    context = (
        jnp.transpose(normalised, (2, 0, 1, 3))
        .reshape(shard_rows, heads_local * HEAD_SIZE)
        .astype(jnp.bfloat16)
    )
    summed = lax.psum_scatter(
        jnp.dot(context, w_out, preferred_element_type=jnp.float32).astype(jnp.bfloat16),
        "req",
        scatter_dimension=0,
        tiled=True,
    ).astype(jnp.float32)
    residual = lax.dynamic_slice_in_dim(tokens, lax.axis_index("req") * half_rows, half_rows, 0)
    hidden = (summed + residual.astype(jnp.float32)).astype(jnp.bfloat16)
    key_value_cache = jnp.stack(
        [
            cache_keys.reshape(slot_count, PAGE_TOKENS, kv_local * HEAD_SIZE),
            cache_values.reshape(slot_count, PAGE_TOKENS, kv_local * HEAD_SIZE),
        ],
        1,
    ).astype(jnp.bfloat16)
    return (hidden, key_value_cache)


def solution(mesh):
    in_specs = (
        P("seq", None),
        P(),
        P(None, "req"),
        P(None, "req"),
        P(None, "req"),
        P("req", None),
        P(),
        P(),
        P(),
    )
    out_specs = (P(("seq", "req"), None), P("seq", None, None, "req"))
    return jax.shard_map(
        on_device, mesh=mesh, in_specs=in_specs, out_specs=out_specs, check_vma=False
    )
```

profile of v0, /device:TPU:1, one launch (start us, length us, event | category | flops | bytes accessed | tf_op | source)
XLA Modules:
  0.0 717.7 jit_solution(10461966883109596945)
XLA Ops:
  8.7 2.4 convolution_convert_fusion.1
  11.3 1.6 fusion.44
  13.0 5.1 select_reduce_fusion
  18.6 101.9 %gather_fusion = s32[16384]{0:T(1024)S(1)} fusion(s32[512]{0:T(512)S(1)} %copy-done.1, s32[16384]{0:T(1024)S(1)} %broadcast_clamp_fusion), kind=kCustom, calls=%fused_computation | custom fusion | bytes 196608 | tf_op jit(solution)/shard_map/gather | solution.py:75
  124.2 2.1 fusion.42
  127.7 107.3 %all-gather.5.cloned.1.call-done = bf16[16384,256]{1,0:T(8,128)(2,1)} async-done(((bf16[128,256]{1,0:T(8,128)(2,1)}), bf16[16384,256]{1,0:T(8,128)(2,1)}) %all-gather.5.cloned.1.call-update) | async-done | bytes 8388624 | tf_op jit(solution)/shard_map/all_gather | solution.py:144
  235.0 222.0 %all-gather.3.cloned.1.call-done = bf16[16384,256]{1,0:T(8,128)(2,1)} async-done(((bf16[128,256]{1,0:T(8,128)(2,1)}), bf16[16384,256]{1,0:T(8,128)(2,1)}) %all-gather.3.cloned.1.call-update) | async-done | bytes 8388624 | tf_op jit(solution)/shard_map/all_gather | solution.py:143
  458.4 211.7 %while.19 = (s32[]{:T(128)}, f32[2,2,128]{2,1,0:T(2,128)S(1)}, f32[2,2,128]{2,1,0:T(2,128)S(1)}, f32[2,2,128,128]{3,2,1,0:T(8,128)}, f32[256,256]{1,0:T(8,128)},...) while((s32[]{:T(128)}, f32[2,2,128]{2,1,0:T(2,128)S(1)}, ...), condition=%wide.region_11.12_spmd.clone, body=%wide.region_5.11_spmd.clone.sunk | while | flops 544936448 | bytes 20653632 | solution.py:170
  463.4 2.1 constant_dynamic-slice_fusion.3
  467.8 3.5 conditional.3
  467.8 1.5 convolution_add_fusion
  469.3 2.0 convolution_add_fusion.1
  479.1 2.1 constant_dynamic-slice_fusion.3
  492.1 2.1 constant_dynamic-slice_fusion.3
  502.2 1.4 compare_reduce_fusion.2
  505.2 2.1 constant_dynamic-slice_fusion.3
  518.3 2.1 constant_dynamic-slice_fusion.3
  528.3 1.4 compare_reduce_fusion.2
  531.4 2.1 constant_dynamic-slice_fusion.3
  544.4 2.1 constant_dynamic-slice_fusion.3
  554.4 1.4 compare_reduce_fusion.2
  557.5 2.1 constant_dynamic-slice_fusion.3
  570.6 2.1 constant_dynamic-slice_fusion.3
  583.7 2.1 constant_dynamic-slice_fusion.3
  596.7 2.1 constant_dynamic-slice_fusion.3
  609.8 2.1 constant_dynamic-slice_fusion.3
  622.9 2.1 constant_dynamic-slice_fusion.3
  636.0 2.1 constant_dynamic-slice_fusion.3
  649.0 2.1 constant_dynamic-slice_fusion.3
  662.1 2.1 constant_dynamic-slice_fusion.3
  673.4 36.1 %reduce-scatter.2.cloned.1.call-done = bf16[64,2048]{1,0:T(8,128)(2,1)} async-done(((bf16[128,2048]{1,0:T(8,128)(2,1)}), bf16[64,2048]{1,0:T(8,128)(2,1)}) %reduce-scatter.2.cloned.1.call-update) | async-done | bytes 262160 | tf_op jit(solution)/shard_map/reduce_scatter | solution.py:181
  709.5 1.7 add_convert_fusion
  (536 shorter events, 160.1 us)
Async XLA Ops:
  7.2 664.1 %copy-start = (bf16[512,2048]{1,0:T(8,128)(2,1)S(1)}, bf16[512,2048]{1,0:T(8,128)(2,1)}, u32[]{:S(2)}) copy-start(bf16[512,2048]{1,0:T(8,128)(2,1)} %param.18) | copy-start | bytes 6291460
  7.2 4.1 copy-start.5
  7.2 4.1 copy-start.13
  7.2 227.8 %all-gather.5.cloned.1.call-start = ((), (), s32[]{:S(2)}) async-start(), calls=%async_computation.2 | async-start | bytes 8454144 | tf_op jit(solution)/shard_map/all_gather | solution.py:144
  8.6 4.4 copy-start.14
  8.7 10.0 %copy-start.1 = (s32[512]{0:T(512)S(1)}, s32[512]{0:T(512)}, u32[]{:S(2)}) copy-start(s32[512]{0:T(512)} %param.21) | copy-start | bytes 6148
  11.1 446.0 %all-gather.3.cloned.1.call-start = ((), (), s32[]{:S(2)}) async-start(), calls=%async_computation.1 | async-start | bytes 8454144 | tf_op jit(solution)/shard_map/all_gather | solution.py:143
  123.5 586.0 %reduce-scatter.2.cloned.1.call-start = ((), (), s32[]{:S(2)}) async-start(), calls=%async_computation.3 | async-start | bytes 786432 | tf_op jit(solution)/shard_map/reduce_scatter | solution.py:181
  474.0 4.0 copy-start.7
  474.0 4.0 copy-start.9
  487.1 4.0 copy-start.9
  500.2 4.0 copy-start.7
  500.2 4.0 copy-start.9
  513.2 4.0 copy-start.9
  526.3 4.0 copy-start.7
  526.3 4.0 copy-start.9
  539.4 4.0 copy-start.9
  552.4 4.0 copy-start.7
  552.4 4.0 copy-start.9
  565.5 4.0 copy-start.7
  565.5 4.0 copy-start.9
  578.6 4.0 copy-start.9
  591.7 4.0 copy-start.7
  591.7 4.0 copy-start.9
  604.7 4.0 copy-start.9
  617.8 4.0 copy-start.7
  617.8 4.0 copy-start.9
  630.9 4.0 copy-start.7
  630.9 4.0 copy-start.9
  644.0 4.0 copy-start.9
  657.0 4.0 copy-start.9
  671.3 38.2 %copy-start.6 = (bf16[128,2048]{1,0:T(8,128)(2,1)S(1)}, bf16[128,2048]{1,0:T(8,128)(2,1)}, u32[]{:S(2)}) copy-start(bf16[128,2048]{1,0:T(8,128)(2,1)} %param.13) | copy-start | bytes 1572868
  (107 other events, 158.1 us)
Sparse Core Ops, SparseCore 0:
  11.2 223.7 all-gather.4
  237.5 219.5 all-gather.2
  672.7 36.6 reduce-scatter.1
where the time goes:
time: 720 us; the launch traced here: 718 us
  waiting for transfers between devices  365 us (51%)
  local copies, waits for them, and re-layouts  222 us (31%)
  other arithmetic  60.5 us (8%)
  matrix products  33.4 us (5%)
  loops' own time  22.3 us (3%)
  between operations  14.1 us (2%)
    all_gather x1, waiting for transfers between devices, on_device(): key_piece = lax.all_gather(key_matrix_rows, 'seq', axis=0, tiled=True)  222 us
    all_gather x1, waiting for transfers between devices, on_device(): value_piece = lax.all_gather(value_matrix_rows, 'seq', axis=0, tiled=True)  107 us
    gather x1, local copies, waits for them, and re-layouts, on_device(): slot_ids = page_slot[position // PAGE_TOKENS]  102 us
    dynamic_slice x32, local copies, waits for them, and re-layouts, sub_step(): value_block = lax.dynamic_slice_in_dim(value_piece, offset, sub_width, 0)  49.8 us
    reduce_scatter x1, waiting for transfers between devices, on_device(): lax.psum_scatter(jnp.dot(context, w_out, preferred_element_type=jnp.float...  36.1 us
    while x272, local copies, waits for them, and re-layouts  25.1 us
    another operation x1, loops' own time, on_device(): lax.scan(sub_step, absorb_state, jnp.arange(length // sub_width, dtype=jn...  22.3 us
    reduce_or x16, other arithmetic, sub_step(): jnp.any(key_target >= 0)  22.2 us
  transfers between devices with their start and end apart: 3, of which 3 were waited for; matrix products, arithmetic and copies ran while one was open for 16% of the time, Pallas kernels for 0%

commit v1 on v0

v1 whole, which is shorter than its diff:
```python
import math

import jax
import jax.numpy as jnp
from jax import lax
from jax.experimental import pallas as pl
from jax.experimental.pallas import tpu as pltpu
from jax.sharding import PartitionSpec as P

MESH = pl.DeviceIdType.MESH
ANY = pl.BlockSpec(memory_space=pl.ANY)
HBM = pl.BlockSpec(memory_space=pltpu.HBM)
VMEM = pl.BlockSpec(memory_space=pltpu.VMEM)
SMEM = pl.BlockSpec(memory_space=pltpu.SMEM)

NY, NX, NZ, NC = 2, 4, 8, 2
NSEQ = NY * NX * NZ * NC
NXY = NX * NY
HEAD = 128
BLOCK = 64
ROWS = 128
PAGE = 32
SLOTS = 8
WIDTH = 2048
QCOLS = 512
KCOLS = 256
THETA = 1000000.0
EPS = 1e-05
FAR = -1e30
FLOOR = -1e29
SCALE2 = math.log2(math.e) / math.sqrt(HEAD)
MIB = 1 << 20
BF16 = jnp.bfloat16
F32 = jnp.float32

STEP = 8
QUAD = 4
KEYS = STEP * BLOCK
LANES = QUAD * 2 * BLOCK
GROUPS = 2 * NXY // QUAD

T_IDX = 0
T_BLK = T_IDX + 64
T_QIDX = T_BLK + 64 + STEP
T_QBLK = T_QIDX + 2 * NXY
T_LO = T_QBLK + 2 * NXY
T_STEPS = T_LO + GROUPS
T_BEGIN = T_STEPS + GROUPS
T_PAGE = T_BEGIN + 4


def coords(d):
    return d // 64, (d // 16) % NX, (d // 2) % NZ, d % 2


def index_of(y, x, z, c):
    return ((y * NX + x) * NZ + z) * NC + c


def plane(y, x, z, c):
    return [
        ((x + i) % NX, y if j == 0 else 1 - y, index_of(y if j == 0 else 1 - y, (x + i) % NX, z, c))
        for j in range(NY)
        for i in range(NX)
    ]


NODES = [(0, 0)]
for _k in (1, 2, 3):
    NODES += [(1, -_k), (1, _k), (0, -_k), (0, _k)]
NODES += [(1, 4), (0, 4)]


def passed_on(own, dz):
    out = []
    if -3 < dz <= 0 or (dz == -3 and own):
        out.append(("up", dz - 1))
    if 0 <= dz < 3 or (dz == 3 and not own):
        out.append(("down", dz + 1))
    return [(to, 4 if abs(to_dz) == 4 else to_dz) for to, to_dz in out]


def gather_kernel(
    tok_hbm, gain_ref, wq_hbm, wk_hbm, wv_hbm, cos_ref, sin_ref, kvall, qall,
    tok, wq, wk, wv, normed, acc, kv, q, load_sem, send_sem, recv_sem, local_sem,
):
    d, r = lax.axis_index("seq"), lax.axis_index("req")
    y, x, z, c = coords(d)
    loads = [pltpu.make_async_copy(tok_hbm, tok, load_sem.at[0])]
    for k in range(4):
        rows = pl.ds(512 * k, 512)
        for n, (src, dst) in enumerate(((wq_hbm, wq), (wk_hbm, wk), (wv_hbm, wv))):
            loads.append(
                pltpu.make_async_copy(src.at[rows], dst.at[rows], load_sem.at[1 + 3 * k + n])
            )
    for copy in loads:
        copy.start()
    near = {
        "sib": index_of(y, x, z, 1 - c),
        "up": index_of(y, x, (z + 1) % NZ, c),
        "down": index_of(y, x, (z + NZ - 1) % NZ, c),
    }
    peers = plane(y, x, z, c)
    barrier = pltpu.get_barrier_semaphore()
    everyone = list(near.values()) + [peer[2] for peer in peers[1:]]
    for peer in everyone:
        pl.semaphore_signal(barrier, inc=1, device_id=(peer, r), device_id_type=MESH)

    loads[0].wait()
    wide = tok[...].astype(F32)
    inv = lax.rsqrt(jnp.mean(wide * wide, -1, keepdims=True) + EPS)
    normed[...] = (wide * inv * gain_ref[...]).astype(BF16)
    for k in range(4):
        for copy in loads[1 + 3 * k : 4 + 3 * k]:
            copy.wait()
        rows = slice(512 * k, 512 * (k + 1))
        part = normed[:, rows]
        for cols, weights in ((slice(0, 512), wq), (slice(512, 768), wk), (slice(768, 1024), wv)):
            value = jnp.dot(part, weights[rows, :], preferred_element_type=F32)
            if k == 0:
                acc[:, cols] = value
            else:
                acc[:, cols] += value
    cosine, sine = cos_ref[...], sin_ref[...]
    for h in range(6):
        u = acc[:, HEAD * h : HEAD * (h + 1)]
        turned = (u * cosine + pltpu.roll(u, HEAD // 2, 1) * sine).astype(BF16)
        if h < 4:
            q[h // 2, :, HEAD * (h % 2) : HEAD * (h % 2 + 1)] = turned
        else:
            kv[h - 4, 0] = turned
    for g in range(2):
        kv[g, 1] = acc[:, 768 + HEAD * g : 768 + HEAD * (g + 1)].astype(BF16)
    pl.semaphore_wait(barrier, len(everyone))

    flying = {}

    def send(name, n, src, dst, to):
        copy = pltpu.make_async_remote_copy(
            src_ref=src,
            dst_ref=dst,
            send_sem=send_sem.at[n],
            recv_sem=recv_sem.at[n],
            device_id=(to, r),
            device_id_type=MESH,
        )
        copy.start()
        flying[name] = copy

    def shard(own, dz):
        return kvall.at[(z + dz + NZ) % NZ, c, y if own else 1 - y]

    def relay(own, dz):
        here = shard(own, dz)
        src = kv.at[y] if (own, dz) == (1, 0) else here
        for to, far in passed_on(own, dz):
            send((own, far), NODES.index((own, far)), src, here, near[to])
        n = len(NODES) + 8 * own + dz % NZ
        send(("s", own, dz), n, src, here, near["sib"])

    relay(1, 0)
    send((0, 0), 0, kv.at[1 - y], shard(1, 0), peers[NX][2])
    for n, (px, py, peer) in enumerate(peers):
        if n:
            send(("q", n), len(NODES) + 15 + n, q.at[py], qall.at[x, y], peer)
    keep = [
        pltpu.make_async_copy(kv.at[y], shard(1, 0), local_sem.at[0]),
        pltpu.make_async_copy(q.at[y], qall.at[x, y], local_sem.at[1]),
    ]
    for copy in keep:
        copy.start()
    for node in NODES:
        flying[node].wait_recv()
        relay(*node)
    for name, copy in flying.items():
        if name[0] in ("s", "q"):
            copy.wait_recv()
    for copy in flying.values():
        copy.wait_send()
    for copy in keep:
        copy.wait()


def gather(tokens, gain, wq, wk, wv, cosine, sine):
    count = len(NODES) + 16 + NXY - 1
    return pl.pallas_call(
        gather_kernel,
        out_shape=(
            jax.ShapeDtypeStruct((NZ, NC, NY, 2, ROWS, HEAD), BF16),
            jax.ShapeDtypeStruct((NX, NY, ROWS, 2 * HEAD), BF16),
        ),
        in_specs=[HBM, VMEM, HBM, HBM, HBM, VMEM, VMEM],
        out_specs=(ANY, ANY),
        scratch_shapes=[
            pltpu.VMEM((ROWS, WIDTH), BF16),
            pltpu.VMEM((WIDTH, QCOLS), BF16),
            pltpu.VMEM((WIDTH, KCOLS), BF16),
            pltpu.VMEM((WIDTH, KCOLS), BF16),
            pltpu.VMEM((ROWS, WIDTH), BF16),
            pltpu.VMEM((ROWS, 1024), F32),
            pltpu.VMEM((2, 2, ROWS, HEAD), BF16),
            pltpu.VMEM((2, ROWS, 2 * HEAD), BF16),
            pltpu.SemaphoreType.DMA((13,)),
            pltpu.SemaphoreType.DMA((count,)),
            pltpu.SemaphoreType.DMA((count,)),
            pltpu.SemaphoreType.DMA((2,)),
        ],
        compiler_params=pltpu.CompilerParams(
            collective_id=1, has_side_effects=True, vmem_limit_bytes=32 * MIB
        ),
        name="gather",
    )(tokens, gain, wq, wk, wv, cosine, sine)


def attend_kernel(
    table, q_ref, kv_ref, o_ref, lse_ref, pages_ref, keys, values, queries, acc, top, total
):
    def block_rows(part, at):
        rows = kv_ref[at // 2, part, pl.ds(at % 2 * 2, 2)]
        return rows.reshape(BLOCK, HEAD)

    def sort_pair(n, _):
        one, two = table[T_IDX + 2 * n], table[T_IDX + 2 * n + 1]
        at = pl.multiple_of(n * 2 * BLOCK, 2 * BLOCK)
        keys[pl.ds(at, BLOCK), :] = block_rows(0, one)
        keys[pl.ds(at + BLOCK, BLOCK), :] = block_rows(0, two)
        pair = jnp.concatenate([block_rows(1, one), block_rows(1, two)], 0)
        values[:, pl.ds(at, 2 * BLOCK)] = jnp.transpose(pair)
        return 0

    lax.fori_loop(0, 32, sort_pair, 0, unroll=4)
    keys[64 * BLOCK :, :] = jnp.zeros((KEYS, HEAD), BF16)
    values[:, 64 * BLOCK :] = jnp.zeros((HEAD, KEYS), BF16)

    def sort_query(n, _):
        at = table[T_QIDX + n]
        rows = q_ref[at // 2, at % 2]
        to = pl.multiple_of(n * 2 * BLOCK, 2 * BLOCK)
        queries[pl.ds(to, BLOCK), :] = rows[:, :HEAD]
        queries[pl.ds(to + BLOCK, BLOCK), :] = rows[:, HEAD:]
        return 0

    lax.fori_loop(0, 2 * NXY, sort_query, 0, unroll=4)

    def pick(n, _):
        at = table[T_PAGE + n]
        for part in range(2):
            pages_ref[n // SLOTS, n % SLOTS, part] = kv_ref[at // 4, part, at % 4]
        return 0

    lax.fori_loop(0, NXY * SLOTS, pick, 0, unroll=4)

    lane = lax.broadcasted_iota(jnp.int32, (1, 2 * BLOCK), 1) % BLOCK
    inner = lax.broadcasted_iota(jnp.int32, (BLOCK, LANES), 0)

    def group(m, _):
        pos = jnp.concatenate(
            [table[T_QBLK + QUAD * m + j] * BLOCK + lane for j in range(QUAD)], 1
        )
        first = jnp.zeros_like(pos)
        for k in range(1, 4):
            begin = table[T_BEGIN + k]
            first = jnp.where(pos >= begin, begin, first)
        mine = queries[pl.ds(pl.multiple_of(m * LANES, LANES), LANES), :]
        lo = table[T_LO + m]
        top[...] = jnp.full_like(top, FLOOR)
        total[...] = jnp.zeros_like(total)
        acc[...] = jnp.zeros_like(acc)

        def step(n, _):
            rank = lo + n * STEP
            at = pl.multiple_of(rank * BLOCK, 2 * BLOCK)
            s = lax.dot_general(
                keys[pl.ds(at, KEYS), :], mine, (((1,), (1,)), ((), ())), preferred_element_type=F32
            )
            pieces = []
            for j in range(STEP):
                base = table[T_BLK + rank + j] * BLOCK
                visible = (inner >= first - base) & (inner <= pos - base)
                pieces.append(jnp.where(visible, s[j * BLOCK : (j + 1) * BLOCK], FAR))
            s = jnp.concatenate(pieces, 0)
            before = top[...]
            higher = jnp.maximum(before, jnp.max(s, 0, keepdims=True))
            e = jnp.exp2((s - higher) * SCALE2)
            fade = jnp.exp2((before - higher) * SCALE2)
            top[...] = higher
            total[...] = total[...] * fade + jnp.sum(e, 0, keepdims=True)
            acc[...] = acc[...] * fade + jnp.dot(
                values[:, pl.ds(at, KEYS)], e.astype(BF16), preferred_element_type=F32
            )
            return 0

        lax.fori_loop(0, table[T_STEPS + m], step, 0)
        seen = total[...] > 0.0
        safe = jnp.where(seen, total[...], 1.0)
        lse = jnp.where(seen, top[...] * SCALE2 + jnp.log2(safe), FAR)
        inverse = 1.0 / safe
        for j in range(QUAD):
            at = table[T_QIDX + QUAD * m + j]
            cols = slice(j * 2 * BLOCK, (j + 1) * 2 * BLOCK)
            out = jnp.transpose(acc[:, cols] * inverse[:, cols]).astype(BF16)
            o_ref[at // 2, at % 2, :, :HEAD] = out[:BLOCK]
            o_ref[at // 2, at % 2, :, HEAD:] = out[BLOCK:]
            lse_ref[at // 2, at % 2] = jnp.broadcast_to(lse[:, cols], (8, 2 * BLOCK))
        return 0

    lax.fori_loop(0, GROUPS, group, 0)


def attend(table, q, kv):
    return pl.pallas_call(
        attend_kernel,
        in_specs=[SMEM, VMEM, VMEM],
        out_specs=(VMEM, VMEM, VMEM),
        out_shape=(
            jax.ShapeDtypeStruct((NXY, 2, BLOCK, 2 * HEAD), BF16),
            jax.ShapeDtypeStruct((NXY, 2, 8, 2 * BLOCK), F32),
            jax.ShapeDtypeStruct((NXY, SLOTS, 2, PAGE, HEAD), BF16),
        ),
        scratch_shapes=[
            pltpu.VMEM((64 * BLOCK + KEYS, HEAD), BF16),
            pltpu.VMEM((HEAD, 64 * BLOCK + KEYS), BF16),
            pltpu.VMEM((2 * NXY * 2 * BLOCK, HEAD), BF16),
            pltpu.VMEM((HEAD, LANES), F32),
            pltpu.VMEM((1, LANES), F32),
            pltpu.VMEM((1, LANES), F32),
        ],
        compiler_params=pltpu.CompilerParams(vmem_limit_bytes=32 * MIB),
        name="attend",
    )(table, q, kv)


CHUNK = 512
CHUNKS = WIDTH // CHUNK


def finish_kernel(
    column, o_ref, lse_ref, pages_ref, w_ref, tok_ref, out_ref, cache_ref,
    held, lses, fetched, weights, tok, context, mine, outgoing, incoming, send_sem, recv_sem, local_sem,
):
    d, r = lax.axis_index("seq"), lax.axis_index("req")
    y, x, z, c = coords(d)
    partner = 1 - r
    local = [
        pltpu.make_async_copy(o_ref.at[x * NY + y], held.at[x, y], local_sem.at[0]),
        pltpu.make_async_copy(lse_ref.at[x * NY + y], lses.at[x, y], local_sem.at[1]),
        pltpu.make_async_copy(w_ref, weights, local_sem.at[2]),
        pltpu.make_async_copy(tok_ref.at[pl.ds(r * BLOCK, BLOCK)], tok, local_sem.at[3]),
        pltpu.make_async_copy(pages_ref.at[x * NY + y], fetched.at[x, y], local_sem.at[4]),
    ]
    for copy in local:
        copy.start()
    peers = plane(y, x, z, c)
    barrier = pltpu.get_barrier_semaphore()
    for _, _, peer in peers[1:]:
        pl.semaphore_signal(barrier, inc=1, device_id=(peer, r), device_id_type=MESH)
    pl.semaphore_signal(barrier, inc=1, device_id=(d, partner), device_id_type=MESH)
    pl.semaphore_wait(barrier, NXY)

    def send(n, src, dst, to):
        copy = pltpu.make_async_remote_copy(
            src_ref=src,
            dst_ref=dst,
            send_sem=send_sem.at[n],
            recv_sem=recv_sem.at[n],
            device_id=to,
            device_id_type=MESH,
        )
        copy.start()
        return copy

    def to_plane(first, src, dst):
        return [
            send(first + n, src.at[px * NY + py], dst.at[x, y], (peer, r))
            for n, (px, py, peer) in enumerate(peers[1:])
        ]

    parts = to_plane(0, lse_ref, lses) + to_plane(7, o_ref, held)
    for copy in local:
        copy.wait()
    for copy in parts:
        copy.wait_recv()
    moved = to_plane(14, pages_ref, fetched)
    eye = lax.broadcasted_iota(jnp.int32, (HEAD, HEAD), 0) == lax.broadcasted_iota(
        jnp.int32, (HEAD, HEAD), 1
    )
    for h in range(2):
        for g in range(NY):
            levels = [lses[i, g, h, 0:1, :] for i in range(NX)]
            top = jnp.maximum(jnp.maximum(levels[0], levels[1]), jnp.maximum(levels[2], levels[3]))
            shares = [jnp.exp2(level - top) for level in levels]
            whole = shares[0] + shares[1] + shares[2] + shares[3]
            columns = [
                jnp.sum(jnp.where(eye, share / whole, 0.0), 1, keepdims=True) for share in shares
            ]
            for a in range(2):
                lanes = slice(a * HEAD, (a + 1) * HEAD)
                value = 0.0
                for i in range(NX):
                    value += columns[i][a * BLOCK : (a + 1) * BLOCK] * held[i, g, h, :, lanes].astype(F32)
                context[h, :, (2 * g + a) * HEAD : (2 * g + a + 1) * HEAD] = value.astype(BF16)
    trades = []
    theirs = context[partner]
    for n in range(CHUNKS):
        cols = slice(n * CHUNK, (n + 1) * CHUNK)
        outgoing[n] = jnp.dot(theirs, weights[:, cols], preferred_element_type=F32).astype(BF16)
        trades.append(send(21 + n, outgoing.at[n], incoming.at[n], (d, partner)))
    ours = context[r]
    for n in range(CHUNKS):
        cols = slice(n * CHUNK, (n + 1) * CHUNK)
        mine[:, cols] = tok[:, cols].astype(F32) + jnp.dot(
            ours, weights[:, cols], preferred_element_type=F32
        )
    for n in range(CHUNKS):
        cols = slice(n * CHUNK, (n + 1) * CHUNK)
        trades[n].wait_recv()
        out_ref[:, cols] = (mine[:, cols] + incoming[n].astype(F32)).astype(BF16)
    for copy in moved:
        copy.wait_recv()
    for j in range(SLOTS):
        at = column[j]
        held_here = jnp.full((2, PAGE, HEAD), at, jnp.int32) >= 0
        source = jnp.maximum(at, 0)
        for g in range(NY):
            page = fetched[source, g, j].astype(F32)
            cache_ref[j, :, :, g * HEAD : (g + 1) * HEAD] = jnp.where(held_here, page, 0.0).astype(BF16)
    for copy in parts + moved + trades:
        copy.wait_send()


def finish(column, o, lse, pages, w_out, tokens):
    count = 21 + CHUNKS
    return pl.pallas_call(
        finish_kernel,
        out_shape=(
            jax.ShapeDtypeStruct((BLOCK, WIDTH), BF16),
            jax.ShapeDtypeStruct((SLOTS, 2, PAGE, KCOLS), BF16),
        ),
        in_specs=[SMEM, ANY, ANY, ANY, HBM, HBM],
        out_specs=(VMEM, VMEM),
        scratch_shapes=[
            pltpu.VMEM((NX, NY, 2, BLOCK, 2 * HEAD), BF16),
            pltpu.VMEM((NX, NY, 2, 8, 2 * BLOCK), F32),
            pltpu.VMEM((NX, NY, SLOTS, 2, PAGE, HEAD), BF16),
            pltpu.VMEM((QCOLS, WIDTH), BF16),
            pltpu.VMEM((BLOCK, WIDTH), BF16),
            pltpu.VMEM((2, BLOCK, QCOLS), BF16),
            pltpu.VMEM((BLOCK, WIDTH), F32),
            pltpu.VMEM((CHUNKS, BLOCK, CHUNK), BF16),
            pltpu.VMEM((CHUNKS, BLOCK, CHUNK), BF16),
            pltpu.SemaphoreType.DMA((count,)),
            pltpu.SemaphoreType.DMA((count,)),
            pltpu.SemaphoreType.DMA((5,)),
        ],
        compiler_params=pltpu.CompilerParams(
            collective_id=2, has_side_effects=True, vmem_limit_bytes=32 * MIB
        ),
        name="finish",
    )(column, o, lse, pages, w_out, tokens)


def chosen(mask, values, axis):
    return jnp.sum(jnp.where(mask, values, 0), axis)


def tables(lengths, block_split, page_slot):
    d = lax.axis_index("seq")
    y, x, z, c = coords(d)
    iota = lambda n: jnp.arange(n, dtype=jnp.int32)
    four = iota(4)
    ends = chosen(four[None, :] <= four[:, None], lengths[None, :], 1)
    begins = ends - lengths

    def start_of(pos):
        return jnp.max(jnp.where(pos[:, None] >= begins[None, :], begins[None, :], 0), 1)

    own = block_split[d]
    pos = jnp.concatenate([own * BLOCK + iota(BLOCK), (2 * NSEQ - 1 - own) * BLOCK + iota(BLOCK)])
    rel = (pos - start_of(pos)).astype(F32)
    inv_freq = jnp.power(THETA, -(jnp.arange(HEAD // 2, dtype=F32) * (2.0 / HEAD)))
    angle = rel[:, None] * inv_freq[None, :]
    cosine, sine = jnp.cos(angle), jnp.sin(angle)
    cosine = jnp.concatenate([cosine, cosine], 1)
    sine = jnp.concatenate([-sine, sine], 1)
    grid = block_split.reshape(NY, NX, NZ, NC)
    line = lax.dynamic_index_in_dim(grid, x, 1, keepdims=False)
    line = jnp.transpose(line, (1, 2, 0)).reshape(32)
    blocks = jnp.stack([line, 2 * NSEQ - 1 - line], 1).reshape(64)
    rank = jnp.sum((blocks[None, :] < blocks[:, None]).astype(jnp.int32), 1)
    hit = rank[None, :] == iota(64)[:, None]
    order = chosen(hit, iota(64)[None, :], 1)
    sorted_blocks = chosen(hit, blocks[None, :], 1)
    beyond = jnp.full((STEP,), 1 << 14, jnp.int32)
    across = jnp.transpose(grid[:, :, z, c]).reshape(NXY)
    qblocks = jnp.stack([across, 2 * NSEQ - 1 - across], 1).reshape(2 * NXY)
    qrank = jnp.sum((qblocks[None, :] < qblocks[:, None]).astype(jnp.int32), 1)
    qhit = qrank[None, :] == iota(2 * NXY)[:, None]
    qorder = chosen(qhit, iota(2 * NXY)[None, :], 1)
    qsorted = chosen(qhit, qblocks[None, :], 1)
    qstart = start_of(qsorted * BLOCK) // BLOCK
    lo = jnp.sum((blocks[None, :] < qstart[:, None]).astype(jnp.int32), 1)
    hi = jnp.sum((blocks[None, :] <= qsorted[:, None]).astype(jnp.int32), 1)
    lo = jnp.min(lo.reshape(GROUPS, QUAD), 1) // 2 * 2
    hi = jnp.max(hi.reshape(GROUPS, QUAD), 1)
    steps = (hi - lo + STEP - 1) // STEP
    devices = index_of(iota(NY)[None, :], iota(NX)[:, None], z, c).reshape(NXY)
    slots = (devices[:, None] * SLOTS + iota(SLOTS)[None, :]).reshape(NXY * SLOTS)
    page = chosen(page_slot[None, :] == slots[:, None], iota(512)[None, :], 1)
    at = chosen(blocks[None, :] == (page // 2)[:, None], iota(64)[None, :], 1)
    sources = at * 2 + page % 2
    table = jnp.concatenate(
        [order, sorted_blocks, beyond, qorder, qsorted, lo, steps, begins, sources]
    )
    my_found = page_slot[None, :] == (d * SLOTS + iota(SLOTS))[:, None]
    my_page = chosen(my_found, iota(512)[None, :], 1)
    my_block = (my_page // 2)[:, None]
    holder = chosen(
        (block_split[None, :] == my_block) | (2 * NSEQ - 1 - block_split[None, :] == my_block),
        iota(NSEQ)[None, :],
        1,
    )
    column = jnp.where(jnp.any(my_found, 1), (holder // 16) % NX, -1)
    return cosine, sine, table, column


def on_device(
    tokens, norm_gain, w_query, key_projection, value_projection, w_out, lengths, block_split, page_slot
):
    cosine, sine, table, column = tables(lengths, block_split, page_slot)
    kvall, qall = gather(
        tokens, norm_gain.reshape(1, WIDTH), w_query, key_projection, value_projection, cosine, sine
    )
    o, lse, pages = attend(
        table, qall.reshape(NXY, 2, BLOCK, 2 * HEAD), kvall.reshape(32, 2, 4, PAGE, HEAD)
    )
    return finish(column, o, lse, pages, w_out, tokens)


def solution(mesh):
    in_specs = (
        P("seq", None),
        P(),
        P(None, "req"),
        P(None, "req"),
        P(None, "req"),
        P("req", None),
        P(),
        P(),
        P(),
    )
    out_specs = (P(("seq", "req"), None), P("seq", None, None, "req"))
    return jax.shard_map(
        on_device, mesh=mesh, in_specs=in_specs, out_specs=out_specs, check_vma=False
    )
```

time: 720 us -> 102 us (0.14)
  waiting for transfers between devices: 365 us -> 0 us
  local copies, waits for them, and re-layouts: 222 us -> 10.7 us
  Pallas kernels: 0 us -> 80.5 us
  other arithmetic: 60.5 us -> 7.69 us
  matrix products: 33.4 us -> 0 us
  loops' own time: 22.3 us -> 0 us
  between operations: 14.1 us -> 2.22 us
    all_gather x2 -> x0, waiting for transfers between devices: 329 us -> none  [the longest x1 222 us: on_device(): key_piece = lax.all_gather(key_matrix_rows, 'seq', axis=0, tiled=True)]
    gather x1 -> x0, local copies, waits for them, and re-layouts: 102 us -> none  [on_device(): slot_ids = page_slot[position // PAGE_TOKENS]]
    dynamic_slice x97 -> x3, local copies, waits for them, and re-layouts: 91.8 us -> 1.56 us  [the longest x1 1.24 us: tables(): own = block_split[d]]
    pallas_call x0 -> x3, Pallas kernels: none -> 80.5 us  [the longest x1 34.3 us: finish(): pl.pallas_call(finish_kernel, out_shape=(jax.ShapeDtypeStruct((BLOCK, WID...]
    reduce_scatter x1 -> x0, waiting for transfers between devices: 36.1 us -> none  [on_device(): lax.psum_scatter(jnp.dot(context, w_out, preferred_element_type=jnp.float...]
    dot_general x38 -> x0, matrix products: 33.4 us -> none  [the longest x16 14.4 us: attend(): jnp.einsum('hgqk,khd->hgqd', weights.astype(jnp.bfloat16), value_heads, p...]
    while x273 -> x0, local copies, waits for them, and re-layouts: 26.2 us -> none
    another operation x17 -> x0, loops' own time: 22.3 us -> none  [the longest x1 22.3 us: on_device(): lax.scan(sub_step, absorb_state, jnp.arange(length // sub_width, dtype=jn...]
  transfers between devices with their start and end apart: 3 -> 0, of which waited for: 3 -> 0; matrix products, arithmetic and copies ran while one was open for 16% -> 0% of each run, Pallas kernels for 0% -> 0%
where the time goes in v1:
time: 102 us; the launch traced here: 101 us
  Pallas kernels  80.5 us (79%)
  local copies, waits for them, and re-layouts  10.7 us (10%)
  other arithmetic  7.69 us (8%)
  between operations  2.22 us (2%)
    pallas_call x1, Pallas kernels, finish(): pl.pallas_call(finish_kernel, out_shape=(jax.ShapeDtypeStruct((BLOCK, WID...  34.3 us
    pallas_call x1, Pallas kernels, gather(): pl.pallas_call(gather_kernel, out_shape=(jax.ShapeDtypeStruct((NZ, NC, NY...  29.7 us
    pallas_call x1, Pallas kernels, attend(): pl.pallas_call(attend_kernel, in_specs=[SMEM, VMEM, VMEM], out_specs=(VME...  16.5 us
    unnamed x16, local copies, waits for them, and re-layouts  7.19 us
    reduce_sum x6, other arithmetic, chosen(): return jnp.sum(jnp.where(mask, values, 0), axis)  3.69 us

profile of v1, /device:TPU:1, one launch (start us, length us, event | category | flops | bytes accessed | tf_op | source)
XLA Modules:
  0.0 101.1 jit_solution(8598843877440775856)
XLA Ops:
  0.7 1.2 %dynamic_slice.12 = s32[1]{0:T(128)} dynamic-slice(s32[128]{0:T(128)} %param.16, s32[]{:T(128)S(6)} %select_n.157), dynamic_slice_sizes={1} | dynamic-slice | bytes 12 | tf_op jit(solution)/shard_map/dynamic_slice | solution.py:477
  3.4 0.8 select_reduce_fusion.9
  4.1 0.7 sub.92
  4.9 0.9 fusion.1
  5.8 0.9 compare_reduce_fusion
  6.7 0.7 broadcast_subtract_fusion.2
  7.4 0.8 select_reduce_fusion.6
  8.5 0.9 select_reduce_fusion
  9.4 0.8 reshape.188
  10.2 0.3 dynamic-slice_reduce_fusion
  10.5 0.1 copy.26
  10.6 0.1 stack_reshape.6
  10.8 0.1 copy.24
  11.1 0.2 convert_reduce_fusion.3
  11.3 0.1 select_reduce_fusion.4
  11.6 0.1 lt.83
  11.7 0.2 convert_reduce_fusion
  11.9 0.2 select_reduce_fusion.1
  12.2 0.2 convert_reduce_fusion.1
  12.4 0.1 reduce_max.28
  12.6 0.1 reduce_min.9
  12.9 0.3 fusion
  13.4 1.0 %copy-done = bf16[128,2048]{1,0:T(8,128)(2,1)S(1)} copy-done((bf16[128,2048]{1,0:T(8,128)(2,1)S(1)}, bf16[128,2048]{1,0:T(8,128)(2,1)}, u32[]{:S(2)}) %copy-start) | copy-done | bytes 524312
  14.4 1.6 %copy-done.2 = bf16[2048,512]{1,0:T(8,128)(2,1)S(1)} copy-done((bf16[2048,512]{1,0:T(8,128)(2,1)S(1)}, bf16[2048,512]{1,0:T(8,128)(2,1)}, u32[]{:S(2)}) %copy-start.2) | copy-done | bytes 2097176
  16.0 1.2 %copy-done.4 = bf16[2048,256]{1,0:T(8,128)(2,1)S(1)} copy-done((bf16[2048,256]{1,0:T(8,128)(2,1)S(1)}, bf16[2048,256]{1,0:T(8,128)(2,1)}, u32[]{:S(2)}) %copy-start.4) | copy-done | bytes 1048600
  17.2 1.2 %copy-done.5 = bf16[2048,256]{1,0:T(8,128)(2,1)S(1)} copy-done((bf16[2048,256]{1,0:T(8,128)(2,1)S(1)}, bf16[2048,256]{1,0:T(8,128)(2,1)}, u32[]{:S(2)}) %copy-start.5) | copy-done | bytes 1048600
  18.5 0.7 copy-done.6
  19.2 29.7 %gather.1 = (bf16[8,2,2,2,128,128]{5,4,3,2,1,0:T(8,128)(2,1)S(1)}, bf16[4,2,128,256]{3,2,1,0:T(8,128)(2,1)S(1)}) custom-call(bf16[128,2048]{1,0:T(8,128)(2,1)S(1)} %copy-done, f32[1,2048]{1,0:T(1,128)S(1)} %bitcast.11, bf16[2048,512]{1,0:T(8,128)(2,1)S(1)} %copy-done.2, bf16[2048,256]{1,0:T(8,128)(2,1)S(1)} %copy-done.4, bf16[2048,256]{1,0:T(8,128)(2,1)S(1)} %copy-done.5, ...), custom_call_target="tpu_custom_call" | custom-call | tf_op jit(solution)/shard_map/gather/pallas_call | solution.py:186
  48.9 16.5 %attend.1 = (bf16[8,2,64,256]{3,2,1,0:T(8,128)(2,1)S(1)}, f32[8,2,8,128]{3,2,1,0:T(8,128)S(1)}, bf16[8,8,2,32,128]{4,3,2,1,0:T(8,128)(2,1)S(1)}) custom-call(s32[244]{0:T(256)S(1)} %concatenate.16.table, bf16[8,2,64,256]{3,2,1,0:T(8,128)(2,1)S(1)} %bitcast.10, bf16[32,2,4,32,128]{4,3,2,1,0:T(8,128)(2,1)S(1)} %bitcast.9), custom_call_target="tpu_custom_call" | custom-call | tf_op jit(solution)/shard_map/attend/pallas_call | solution.py:311
  65.5 34.3 %finish.1 = (bf16[64,2048]{1,0:T(8,128)(2,1)S(1)}, bf16[8,2,32,256]{3,2,1,0:T(8,128)(2,1)S(1)}) custom-call(s32[8]{0:T(128)S(1)} %fusion.2.column, bf16[8,2,64,256]{3,2,1,0:T(8,128)(2,1)S(1)} %get-tuple-element.9.o_ref, f32[8,2,8,128]{3,2,1,0:T(8,128)S(1)} %get-tuple-element.10.lse_ref, bf16[8,8,2,32,128]{4,3,2,1,0:T(8,128)(2,1)S(1)} %get-tuple-element.11.pages_ref, ...), custom_call_target="tpu_custom_call" | custom-call | tf_op jit(solution)/shard_map/finish/pallas_call | solution.py:433
  99.7 0.7 copy.29
  100.4 0.7 copy.30
  (43 shorter events, 1.5 us)
Async XLA Ops:
  13.4 1.0 %copy-start = (bf16[128,2048]{1,0:T(8,128)(2,1)S(1)}, bf16[128,2048]{1,0:T(8,128)(2,1)}, u32[]{:S(2)}) copy-start(bf16[128,2048]{1,0:T(8,128)(2,1)} %tok_ref.1) | copy-start | bytes 1572868
  14.4 1.6 %copy-start.2 = (bf16[2048,512]{1,0:T(8,128)(2,1)S(1)}, bf16[2048,512]{1,0:T(8,128)(2,1)}, u32[]{:S(2)}) copy-start(bf16[2048,512]{1,0:T(8,128)(2,1)} %wq_hbm.1) | copy-start | bytes 6291460
  16.0 1.2 %copy-start.4 = (bf16[2048,256]{1,0:T(8,128)(2,1)S(1)}, bf16[2048,256]{1,0:T(8,128)(2,1)}, u32[]{:S(2)}) copy-start(bf16[2048,256]{1,0:T(8,128)(2,1)} %wk_hbm.1) | copy-start | bytes 3145732
  17.2 1.2 %copy-start.5 = (bf16[2048,256]{1,0:T(8,128)(2,1)S(1)}, bf16[2048,256]{1,0:T(8,128)(2,1)}, u32[]{:S(2)}) copy-start(bf16[2048,256]{1,0:T(8,128)(2,1)} %wv_hbm.1) | copy-start | bytes 3145732
  18.5 0.7 copy-start.6
  48.9 16.6 %copy-start.1 = (bf16[128,2048]{1,0:T(8,128)(2,1)S(1)}, bf16[128,2048]{1,0:T(8,128)(2,1)}, u32[]{:S(2)}) copy-start(bf16[128,2048]{1,0:T(8,128)(2,1)} %tok_ref.1) | copy-start | bytes 1572868
  48.9 16.6 %copy-start.3 = (bf16[512,2048]{1,0:T(8,128)(2,1)S(1)}, bf16[512,2048]{1,0:T(8,128)(2,1)}, u32[]{:S(2)}) copy-start(bf16[512,2048]{1,0:T(8,128)(2,1)} %w_ref.1) | copy-start | bytes 6291460

commit v2 on v0

v2 whole, which is shorter than its diff:
```python
import math

import jax
import jax.numpy as jnp
import numpy as np
from jax import lax
from jax.experimental import pallas as pl
from jax.experimental.pallas import tpu as pltpu
from jax.sharding import PartitionSpec as P

MESH = pl.DeviceIdType.MESH
ANY = pl.BlockSpec(memory_space=pl.ANY)
HBM = pl.BlockSpec(memory_space=pltpu.HBM)
VMEM = pl.BlockSpec(memory_space=pltpu.VMEM)
SMEM = pl.BlockSpec(memory_space=pltpu.SMEM)

NY, NX, NZ, NC = 2, 4, 8, 2
NSEQ = NY * NX * NZ * NC
NXY = NX * NY
HEAD = 128
BLOCK = 64
ROWS = 128
PAGE = 32
SLOTS = 8
WIDTH = 2048
QCOLS = 512
KCOLS = 256
THETA = 1000000.0
EPS = 1e-05
FAR = -1e30
FLOOR = -1e29
SCALE2 = math.log2(math.e) / math.sqrt(HEAD)
MIB = 1 << 20
BF16 = jnp.bfloat16
F32 = jnp.float32

EXTRA = 16
KEYS = NC * NY * ROWS
LANES = NXY * 2 * ROWS
BEYOND = 1 << 14
CHUNK = 512
CHUNKS = WIDTH // CHUNK

FREQ = np.power(
    np.float32(THETA), -(np.arange(HEAD // 2, dtype=np.float32) * np.float32(2.0 / HEAD))
).astype(np.float32)
FREQ = np.concatenate([FREQ, FREQ])[None, :]


def coords(d):
    return d // 64, (d // 16) % NX, (d // 2) % NZ, d % 2


def index_of(y, x, z, c):
    return ((y * NX + x) * NZ + z) * NC + c


def plane(y, x, z, c):
    return [
        ((x + i) % NX, y if j == 0 else 1 - y, index_of(y if j == 0 else 1 - y, (x + i) % NX, z, c))
        for j in range(NY)
        for i in range(NX)
    ]


NODES = [(0, 0)]
for _k in (1, 2, 3):
    NODES += [(1, -_k), (1, _k), (0, -_k), (0, _k)]
NODES += [(1, 4), (0, 4)]


def passed_on(own, dz):
    out = []
    if -3 < dz <= 0 or (dz == -3 and own):
        out.append(("up", dz - 1))
    if 0 <= dz < 3 or (dz == 3 and not own):
        out.append(("down", dz + 1))
    return [(to, 4 if abs(to_dz) == 4 else to_dz) for to, to_dz in out]


def prompt_start(pos, begins):
    first = jnp.zeros_like(pos)
    for begin in begins:
        first = jnp.where(pos >= begin, begin, first)
    return first


def begins_of(lengths):
    one = lengths[0]
    two = one + lengths[1]
    return one, two, two + lengths[2]


def rotation(own, begins, freq):
    row = lax.broadcasted_iota(jnp.int32, (ROWS, HEAD), 0)
    pos = jnp.where(
        row < BLOCK, own * BLOCK + row, (2 * NSEQ - 1 - own) * BLOCK + row - BLOCK
    )
    angle = (pos - prompt_start(pos, begins)).astype(F32) * freq
    turns = jnp.floor(angle * (2.0 / math.pi) + 0.5)
    rest = angle - turns * 1.5703125
    rest = rest - turns * 4.837512969970703125e-4
    rest = rest - turns * 7.54978995489188216e-8
    quarter = turns.astype(jnp.int32) & 3
    sq = rest * rest
    sine = rest + rest * sq * (-1.6666654611e-1 + sq * (8.3321608736e-3 - sq * 1.9515295891e-4))
    cosine = (
        1.0
        - 0.5 * sq
        + sq * sq * (4.166664568298827e-2 + sq * (-1.388731625493765e-3 + sq * 2.443315711809948e-5))
    )
    odd = (quarter & 1) == 1
    turned_sine = jnp.where(odd, cosine, sine)
    turned_cosine = jnp.where(odd, sine, cosine)
    lower = lax.broadcasted_iota(jnp.int32, (ROWS, HEAD), 1) < HEAD // 2
    minus = (quarter >= 2) != lower
    sine = jnp.where(minus, -turned_sine, turned_sine)
    cosine = jnp.where((quarter == 1) | (quarter == 2), -turned_cosine, turned_cosine)
    return cosine, sine


def diagonal():
    return lax.broadcasted_iota(jnp.int32, (HEAD, HEAD), 0) == lax.broadcasted_iota(
        jnp.int32, (HEAD, HEAD), 1
    )


def stand(row, eye):
    return jnp.sum(jnp.where(eye, jnp.broadcast_to(row, (HEAD, HEAD)), 0.0), 1, keepdims=True)


def table_kernel(split_ref, slot_ref, table_ref):
    y, x, z, c = coords(lax.axis_index("seq"))
    eye = diagonal()
    sub = lax.broadcasted_iota(jnp.int32, (HEAD, HEAD), 0)
    row_lane = lax.broadcasted_iota(jnp.int32, (1, HEAD), 1)

    def pick(mask, value):
        return jnp.sum(jnp.where(mask, value, 0.0), 0, keepdims=True)

    ys, xs, zs, cs = coords(sub)
    split_col = jnp.broadcast_to(stand(split_ref[...].astype(F32), eye), (HEAD, HEAD))
    halves = (split_col, 2 * NSEQ - 1 - split_col)
    place = row_lane // SLOTS % NXY
    wanted = index_of(place % NY, place // NY, z, c) * SLOTS + row_lane % SLOTS
    page, found = 0.0, 0.0
    for k in range(4):
        slots = jnp.broadcast_to(stand(slot_ref[k : k + 1, :].astype(F32), eye), (HEAD, HEAD))
        hit = slots == wanted.astype(F32)
        page += pick(hit, (sub + HEAD * k).astype(F32))
        found += pick(hit, 1.0)
    page = page.astype(jnp.int32)
    block = (page // 2).astype(F32)
    at, column = 0.0, 0.0
    for h in range(2):
        hit = halves[h] == block
        at += pick(hit & (xs == x), (2 * ((zs * NC + cs) * NY + ys) + h).astype(F32))
        column += pick(hit, xs.astype(F32))
    table_ref[0:1, :] = at.astype(jnp.int32) * 2 + page % 2
    table_ref[1:2, :] = jnp.where(found > 0.5, column, -1.0).astype(jnp.int32)
    table_ref[2:, :] = jnp.zeros((6, HEAD), jnp.int32)


def make_table(block_split, page_slot):
    return pl.pallas_call(
        table_kernel,
        out_shape=jax.ShapeDtypeStruct((8, HEAD), jnp.int32),
        in_specs=[VMEM, VMEM],
        out_specs=VMEM,
        name="table",
    )(block_split.reshape(1, NSEQ), page_slot.reshape(4, HEAD))


NODES = [(0, 0)]
for _k in (1, 2, 3):
    NODES += [(1, -_k), (1, _k), (0, -_k), (0, _k)]
NODES += [(1, 4), (0, 4)]
PLACES = [(own, dz) for own in (1, 0) for dz in (0, -1, 1, -2, 2, -3, 3, 4)]


def passed_on(own, dz):
    out = []
    if -3 < dz <= 0 or (dz == -3 and own):
        out.append(("up", dz - 1))
    if 0 <= dz < 3 or (dz == 3 and not own):
        out.append(("down", dz + 1))
    return [(to, 4 if abs(to_dz) == 4 else to_dz) for to, to_dz in out]


def layer_kernel(
    lengths, split, table, tok_hbm, gain_ref, wq_hbm, wk_hbm, wv_hbm, wo_hbm, freq_ref,
    out_ref, cache_ref,
    tok, wq, wk, wv, wo, normed, proj, kv, q, kvall, qall, turned, acc, top,
    parts, levels, held, lses, pages, fetched, context, mine, outgoing, incoming,
    load_sem, send_sem, recv_sem,
):
    d, r = lax.axis_index("seq"), lax.axis_index("req")
    y, x, z, c = coords(d)
    partner = 1 - r
    loads = [pltpu.make_async_copy(tok_hbm, tok, load_sem.at[0])]
    for k in range(4):
        rows = pl.ds(512 * k, 512)
        for n, (src, dst) in enumerate(((wq_hbm, wq), (wk_hbm, wk), (wv_hbm, wv))):
            loads.append(
                pltpu.make_async_copy(src.at[rows], dst.at[rows], load_sem.at[1 + 3 * k + n])
            )
    load_wo = pltpu.make_async_copy(wo_hbm, wo, load_sem.at[13])
    for copy in loads + [load_wo]:
        copy.start()
    near = {
        "sib": (index_of(y, x, z, 1 - c), r),
        "up": (index_of(y, x, (z + 1) % NZ, c), r),
        "down": (index_of(y, x, (z + NZ - 1) % NZ, c), r),
        "req": (d, partner),
    }
    peers = plane(y, x, z, c)
    barrier = pltpu.get_barrier_semaphore()
    everyone = list(near.values()) + [(peer[2], r) for peer in peers[1:]]
    for peer in everyone:
        pl.semaphore_signal(barrier, inc=1, device_id=peer, device_id_type=MESH)

    copies = {}

    def plan(name, src, dst, to):
        n = len(copies)
        copies[name] = pltpu.make_async_remote_copy(
            src_ref=src,
            dst_ref=dst,
            send_sem=send_sem.at[n],
            recv_sem=recv_sem.at[n],
            device_id=to,
            device_id_type=MESH,
        )

    def shard(own, dz):
        return kvall.at[(z + dz + NZ) % NZ, c, y if own else 1 - y]

    plan((0, 0), kv.at[1 - y], shard(1, 0), (peers[NX][2], r))
    for own, dz in PLACES:
        for to, far in passed_on(own, dz):
            plan((own, far), shard(own, dz), shard(own, dz), near[to])
        plan(("s", own, dz), shard(own, dz), shard(own, dz), near["sib"])
    for n, (px, py, peer) in enumerate(peers):
        if n:
            to = (peer, r)
            plan(("q", n), q.at[py], qall.at[x, y], to)
            plan(("l", n), levels.at[px * NY + py], lses.at[x, y], to)
            plan(("o", n), parts.at[px * NY + py], held.at[x, y], to)
            plan(("p", n), pages.at[px * NY + py], fetched.at[x, y], to)
    for n in range(CHUNKS):
        plan(("t", n), outgoing.at[n], incoming.at[n], near["req"])
    others = range(1, NXY)

    def relay(*nodes):
        for own, dz in nodes:
            if (own, dz) != (1, 0):
                copies[own, dz].wait_recv()
            for _, far in passed_on(own, dz):
                copies[own, far].start()
            copies["s", own, dz].start()

    begins = begins_of(lengths)
    cosine, sine = rotation(split[d], begins, freq_ref[...])
    loads[0].wait()
    wide = tok[...].astype(F32)
    inv = lax.rsqrt(jnp.mean(wide * wide, -1, keepdims=True) + EPS)
    normed[...] = (wide * inv * gain_ref[...]).astype(BF16)
    for k in range(4):
        for copy in loads[1 + 3 * k : 4 + 3 * k]:
            copy.wait()
        rows = slice(512 * k, 512 * (k + 1))
        part = normed[:, rows]
        for cols, weights in ((slice(0, 512), wq), (slice(512, 768), wk), (slice(768, 1024), wv)):
            value = jnp.dot(part, weights[rows, :], preferred_element_type=F32)
            if k == 0:
                proj[:, cols] = value
            else:
                proj[:, cols] += value
    for h in range(6):
        u = proj[:, HEAD * h : HEAD * (h + 1)]
        rotated = (u * cosine + pltpu.roll(u, HEAD // 2, 1) * sine).astype(BF16)
        if h < 4:
            q[h // 2, h % 2] = rotated
        else:
            kv[h - 4, 0] = rotated.reshape(4, PAGE, HEAD)
    for g in range(2):
        kv[g, 1] = proj[:, 768 + HEAD * g : 768 + HEAD * (g + 1)].astype(BF16).reshape(4, PAGE, HEAD)
    kvall[z, c, y] = kv[y]
    qall[x, y] = q[y]
    pl.semaphore_wait(barrier, len(everyone))
    relay((1, 0))
    copies[0, 0].start()
    for n in others:
        copies["q", n].start()

    lane = lax.broadcasted_iota(jnp.int32, (1, ROWS), 1)
    pos = []
    for px in range(NX):
        for py in range(NY):
            block = split[index_of(py, px, z, c)]
            row = jnp.where(
                lane < BLOCK, block * BLOCK + lane, (2 * NSEQ - 1 - block) * BLOCK + lane - BLOCK
            )
            pos += [row, row]
    pos = jnp.concatenate(pos, 1)
    first = prompt_start(pos, begins)
    turned[HEAD:, :] = jnp.ones((EXTRA, KEYS), BF16)
    top[...] = jnp.full_like(top, FLOOR)
    acc[...] = jnp.zeros_like(acc)
    inner = lax.broadcasted_iota(jnp.int32, (BLOCK, LANES), 0)

    def build_pages():
        def one(n, _):
            at = table[0, n]
            for part in range(2):
                pages[n // SLOTS, n % SLOTS, part] = kvall[
                    at // 16, at // 8 % 2, at // 4 % 2, part, at % 4
                ]
            return 0

        lax.fori_loop(0, NXY * SLOTS, one, 0)

    def sibling(*places):
        for own, dz in places:
            copies["s", own, dz].wait_recv()

    def batch(i, _):
        @pl.when(i == 0)
        def _():
            relay((0, 0), (1, -1), (1, 1))
            relay((1, -2), (1, 2), (0, -1), (0, 1))
            sibling((1, 0), (0, 0))
            for n in others:
                copies["q", n].wait_recv()

        @pl.when(i == 1)
        def _():
            sibling((1, -1), (0, -1))

        @pl.when(i == 2)
        def _():
            relay((1, -3), (1, 3), (0, -2), (0, 2))
            sibling((1, 1), (0, 1))

        @pl.when(i == 3)
        def _():
            sibling((1, -2), (0, -2))

        @pl.when(i == 4)
        def _():
            relay((1, 4), (0, -3), (0, 3))
            sibling((1, 2), (0, 2))

        @pl.when(i == 5)
        def _():
            sibling((1, -3), (0, -3))

        @pl.when(i == 6)
        def _():
            relay((0, 4))
            sibling((1, 3), (0, 3))

        @pl.when(i == 7)
        def _():
            sibling((1, 4), (0, 4))
            build_pages()
            for n in range(1, NX):
                copies["p", n].start()

        half = (i + 1) // 2
        far = (z + NZ + half * (1 - i % 2 * 2)) % NZ
        pieces = [(cc, yy) for cc in range(NC) for yy in range(NY)]
        for n, (cc, yy) in enumerate(pieces):
            turned[:HEAD, n * ROWS : (n + 1) * ROWS] = jnp.transpose(
                kvall[far, cc, yy, 1].reshape(ROWS, HEAD)
            )
        keys = jnp.concatenate([kvall[far, cc, yy, 0].reshape(ROWS, HEAD) for cc, yy in pieces], 0)
        queries = qall[...].reshape(LANES, HEAD)
        s = lax.dot_general(keys, queries, (((1,), (1,)), ((), ())), preferred_element_type=F32)
        masked = []
        for n, (cc, yy) in enumerate(pieces):
            block = split[index_of(yy, x, far, cc)]
            for h in range(2):
                base = (block if h == 0 else 2 * NSEQ - 1 - block) * BLOCK
                visible = (inner >= first - base) & (inner <= pos - base)
                at = n * ROWS + h * BLOCK
                masked.append(jnp.where(visible, s[at : at + BLOCK], FAR))
        s = jnp.concatenate(masked, 0)
        before = top[...]
        higher = jnp.maximum(before, jnp.max(s, 0, keepdims=True))
        e = jnp.exp2((s - higher) * SCALE2).astype(BF16)
        fade = jnp.exp2((before - higher) * SCALE2)
        top[...] = higher
        acc[...] = acc[...] * fade + jnp.dot(turned[...], e, preferred_element_type=F32)
        return 0

    lax.fori_loop(0, NZ, batch, 0)

    total = acc[HEAD : HEAD + 1, :]
    seen = total > 0.0
    safe = jnp.where(seen, total, 1.0)
    lse = jnp.where(seen, top[...] * SCALE2 + jnp.log2(safe), FAR)
    inverse = 1.0 / safe
    for n in range(NXY):
        cols = slice(n * 2 * ROWS, (n + 1) * 2 * ROWS)
        parts[n] = (acc[:HEAD, cols] * inverse[:, cols]).astype(BF16)
        levels[n] = jnp.broadcast_to(lse[:, cols], (8, 2 * ROWS))
    for n in others:
        copies["l", n].start()
        copies["o", n].start()
    held[x, y] = parts[x * NY + y]
    lses[x, y] = levels[x * NY + y]
    fetched[x, y] = pages[x * NY + y]
    load_wo.wait()
    for n in others:
        copies["l", n].wait_send()
        copies["o", n].wait_send()
    for n in range(NX, NXY):
        copies["p", n].start()
    for n in others:
        copies["l", n].wait_recv()
        copies["o", n].wait_recv()
    for g in range(NY):
        rows = [lses[i, g, 0:1, :] for i in range(NX)]
        peak = jnp.maximum(jnp.maximum(rows[0], rows[1]), jnp.maximum(rows[2], rows[3]))
        shares = [jnp.exp2(row - peak) for row in rows]
        whole = shares[0] + shares[1] + shares[2] + shares[3]
        value = 0.0
        for i in range(NX):
            value += held[i, g].astype(F32) * (shares[i] / whole)
        for a in range(2):
            cols = slice((2 * g + a) * HEAD, (2 * g + a + 1) * HEAD)
            rows = jnp.transpose(value[:, a * ROWS : (a + 1) * ROWS].astype(BF16))
            context[0, :, cols] = rows[:BLOCK]
            context[1, :, cols] = rows[BLOCK:]

    theirs = context[partner]
    for n in range(CHUNKS):
        cols = slice(n * CHUNK, (n + 1) * CHUNK)
        outgoing[n] = jnp.dot(theirs, wo[:, cols], preferred_element_type=F32).astype(BF16)
        copies["t", n].start()
    ours = context[r]
    residual = tok[pl.ds(pl.multiple_of(r * BLOCK, BLOCK), BLOCK), :]
    for n in range(CHUNKS):
        cols = slice(n * CHUNK, (n + 1) * CHUNK)
        mine[:, cols] = residual[:, cols].astype(F32) + jnp.dot(
            ours, wo[:, cols], preferred_element_type=F32
        )
    for n in range(CHUNKS):
        cols = slice(n * CHUNK, (n + 1) * CHUNK)
        copies["t", n].wait_recv()
        out_ref[:, cols] = (mine[:, cols] + incoming[n].astype(F32)).astype(BF16)
    for n in others:
        copies["p", n].wait_recv()
    for j in range(SLOTS):
        at = table[1, (x * NY + y) * SLOTS + j]
        here = jnp.full((2, PAGE, HEAD), at, jnp.int32) >= 0
        source = jnp.maximum(at, 0)
        for g in range(NY):
            page = fetched[source, g, j].astype(F32)
            cache_ref[j, :, :, g * HEAD : (g + 1) * HEAD] = jnp.where(here, page, 0.0).astype(BF16)
    for name, copy in copies.items():
        if name[0] not in ("l", "o"):
            copy.wait_send()


COPIES = 15 + 16 + 4 * (NXY - 1) + CHUNKS


def on_device(
    tokens, norm_gain, w_query, key_projection, value_projection, w_out, lengths, block_split, page_slot
):
    return pl.pallas_call(
        layer_kernel,
        out_shape=(
            jax.ShapeDtypeStruct((BLOCK, WIDTH), BF16),
            jax.ShapeDtypeStruct((SLOTS, 2, PAGE, KCOLS), BF16),
        ),
        in_specs=[SMEM, SMEM, SMEM, HBM, VMEM, HBM, HBM, HBM, HBM, VMEM],
        out_specs=(VMEM, VMEM),
        scratch_shapes=[
            pltpu.VMEM((ROWS, WIDTH), BF16),
            pltpu.VMEM((WIDTH, QCOLS), BF16),
            pltpu.VMEM((WIDTH, KCOLS), BF16),
            pltpu.VMEM((WIDTH, KCOLS), BF16),
            pltpu.VMEM((QCOLS, WIDTH), BF16),
            pltpu.VMEM((ROWS, WIDTH), BF16),
            pltpu.VMEM((ROWS, 1024), F32),
            pltpu.VMEM((2, 2, 4, PAGE, HEAD), BF16),
            pltpu.VMEM((2, 2, ROWS, HEAD), BF16),
            pltpu.VMEM((NZ, NC, NY, 2, 4, PAGE, HEAD), BF16),
            pltpu.VMEM((NX, NY, 2, ROWS, HEAD), BF16),
            pltpu.VMEM((HEAD + EXTRA, KEYS), BF16),
            pltpu.VMEM((HEAD + EXTRA, LANES), F32),
            pltpu.VMEM((1, LANES), F32),
            pltpu.VMEM((NXY, HEAD, 2 * ROWS), BF16),
            pltpu.VMEM((NXY, 8, 2 * ROWS), F32),
            pltpu.VMEM((NX, NY, HEAD, 2 * ROWS), BF16),
            pltpu.VMEM((NX, NY, 8, 2 * ROWS), F32),
            pltpu.VMEM((NXY, SLOTS, 2, PAGE, HEAD), BF16),
            pltpu.VMEM((NX, NY, SLOTS, 2, PAGE, HEAD), BF16),
            pltpu.VMEM((2, BLOCK, QCOLS), BF16),
            pltpu.VMEM((BLOCK, WIDTH), F32),
            pltpu.VMEM((CHUNKS, BLOCK, CHUNK), BF16),
            pltpu.VMEM((CHUNKS, BLOCK, CHUNK), BF16),
            pltpu.SemaphoreType.DMA((14,)),
            pltpu.SemaphoreType.DMA((COPIES,)),
            pltpu.SemaphoreType.DMA((COPIES,)),
        ],
        compiler_params=pltpu.CompilerParams(
            collective_id=1, has_side_effects=True, vmem_limit_bytes=60 * MIB
        ),
        name="layer",
    )(
        lengths, block_split, make_table(block_split, page_slot), tokens, norm_gain.reshape(1, WIDTH), w_query,
        key_projection, value_projection, w_out, jnp.asarray(FREQ),
    )


def solution(mesh):
    in_specs = (
        P("seq", None),
        P(),
        P(None, "req"),
        P(None, "req"),
        P(None, "req"),
        P("req", None),
        P(),
        P(),
        P(),
    )
    out_specs = (P(("seq", "req"), None), P("seq", None, None, "req"))
    return jax.shard_map(
        on_device, mesh=mesh, in_specs=in_specs, out_specs=out_specs, check_vma=False
    )
```

time: 720 us -> 78.5 us (0.11)
  waiting for transfers between devices: 365 us -> 0 us
  local copies, waits for them, and re-layouts: 222 us -> 3.34 us
  Pallas kernels: 0 us -> 74.3 us
  other arithmetic: 60.5 us -> 0 us
  matrix products: 33.4 us -> 0 us
  loops' own time: 22.3 us -> 0 us
  between operations: 14.1 us -> 0.64 us
    all_gather x2 -> x0, waiting for transfers between devices: 329 us -> none  [the longest x1 222 us: on_device(): key_piece = lax.all_gather(key_matrix_rows, 'seq', axis=0, tiled=True)]
    gather x1 -> x0, local copies, waits for them, and re-layouts: 102 us -> none  [on_device(): slot_ids = page_slot[position // PAGE_TOKENS]]
    dynamic_slice x97 -> x0, local copies, waits for them, and re-layouts: 91.8 us -> none  [the longest x32 49.8 us: sub_step(): value_block = lax.dynamic_slice_in_dim(value_piece, offset, sub_width, 0)]
    pallas_call x0 -> x2, Pallas kernels: none -> 74.3 us  [the longest x1 72.8 us: on_device(): pl.pallas_call(layer_kernel, out_shape=(jax.ShapeDtypeStruct((BLOCK, WIDT...]
    reduce_scatter x1 -> x0, waiting for transfers between devices: 36.1 us -> none  [on_device(): lax.psum_scatter(jnp.dot(context, w_out, preferred_element_type=jnp.float...]
    dot_general x38 -> x0, matrix products: 33.4 us -> none  [the longest x16 14.4 us: attend(): jnp.einsum('hgqk,khd->hgqd', weights.astype(jnp.bfloat16), value_heads, p...]
    while x273 -> x0, local copies, waits for them, and re-layouts: 26.2 us -> none
    another operation x17 -> x0, loops' own time: 22.3 us -> none  [the longest x1 22.3 us: on_device(): lax.scan(sub_step, absorb_state, jnp.arange(length // sub_width, dtype=jn...]
  transfers between devices with their start and end apart: 3 -> 0, of which waited for: 3 -> 0; matrix products, arithmetic and copies ran while one was open for 16% -> 0% of each run, Pallas kernels for 0% -> 0%
where the time goes in v2:
time: 78.5 us; the launch traced here: 78.3 us
  Pallas kernels  74.3 us (95%)
  local copies, waits for them, and re-layouts  3.34 us (4%)
    pallas_call x1, Pallas kernels, on_device(): pl.pallas_call(layer_kernel, out_shape=(jax.ShapeDtypeStruct((BLOCK, WIDT...  72.8 us
    unnamed x2, local copies, waits for them, and re-layouts  3.34 us

profile of v2, /device:TPU:1, one launch (start us, length us, event | category | flops | bytes accessed | tf_op | source)
XLA Modules:
  0.0 78.3 jit_solution(5618754074124432576)
XLA Ops:
  0.6 1.5 %table.1 = s32[8,128]{1,0:T(8,128)} custom-call(s32[1,128]{1,0:T(1,128)} %bitcast.5, s32[4,128]{1,0:T(4,128)} %bitcast.4), custom_call_target="tpu_custom_call" | custom-call | tf_op jit(solution)/shard_map/table/pallas_call | solution.py:165
  2.2 72.8 %layer.1 = (bf16[64,2048]{1,0:T(8,128)(2,1)}, bf16[8,2,32,256]{3,2,1,0:T(8,128)(2,1)}) custom-call(s32[4]{0:T(128)} %lengths.1, s32[128]{0:T(128)} %split.1, s32[8,128]{1,0:T(8,128)} %table.1, bf16[128,2048]{1,0:T(8,128)(2,1)} %tok_hbm.1, f32[1,2048]{1,0:T(1,128)} %bitcast.3, bf16[2048,512]{1,0:T(8,128)(2,1)} %wq_hbm.1, bf16[2048,256]{1,0:T(8,128)(2,1)} %wk_hbm.1, ...), custom_call_target="tpu_custom_call" | custom-call | tf_op jit(solution)/shard_map/layer/pallas_call | solution.py:473
  74.9 1.7 %copy.14 = bf16[64,2048]{1,0:T(8,128)(2,1)} copy(bf16[64,2048]{1,0:T(8,128)(2,1)} %get-tuple-element.4) | data formatting | bytes 524288
  76.6 1.7 %copy.15 = bf16[8,2,32,256]{3,2,1,0:T(8,128)(2,1)} copy(bf16[8,2,32,256]{3,2,1,0:T(8,128)(2,1)} %get-tuple-element.5) | data formatting | bytes 524288

commit v3 on v2

--- a/solution.py
+++ b/solution.py
@@ -191,7 +191,7 @@
     lengths, split, table, tok_hbm, gain_ref, wq_hbm, wk_hbm, wv_hbm, wo_hbm, freq_ref,
     out_ref, cache_ref,
     tok, wq, wk, wv, wo, normed, proj, kv, q, kvall, qall, turned, acc, top,
-    parts, levels, held, lses, pages, fetched, context, mine, outgoing, incoming,
+    parts, levels, held, lses, pages, fetched, swapped, swapping, context, mine, outgoing, incoming,
     load_sem, send_sem, recv_sem,
 ):
     d, r = lax.axis_index("seq"), lax.axis_index("req")
@@ -246,9 +246,11 @@
             plan(("q", n), q.at[py], qall.at[x, y], to)
             plan(("l", n), levels.at[px * NY + py], lses.at[x, y], to)
             plan(("o", n), parts.at[px * NY + py], held.at[x, y], to)
-            plan(("p", n), pages.at[px * NY + py], fetched.at[x, y], to)
+            if n < NX:
+                plan(("p", n), pages.at[pl.ds(px * NY, NY)], fetched.at[x], to)
     for n in range(CHUNKS):
         plan(("t", n), outgoing.at[n], incoming.at[n], near["req"])
+    plan(("w", 0), swapped, swapping, (peers[NX][2], r))
     others = range(1, NXY)
 
     def relay(*nodes):
@@ -364,8 +366,8 @@
         def _():
             sibling((1, 4), (0, 4))
             build_pages()
-            for n in range(1, NX):
-                copies["p", n].start()
+            copies["p", 1].start()
+            copies["p", 3].start()
 
         half = (i + 1) // 2
         far = (z + NZ + half * (1 - i % 2 * 2)) % NZ
@@ -410,13 +412,12 @@
         copies["o", n].start()
     held[x, y] = parts[x * NY + y]
     lses[x, y] = levels[x * NY + y]
-    fetched[x, y] = pages[x * NY + y]
+    fetched[x] = pages[pl.ds(x * NY, NY)]
     load_wo.wait()
     for n in others:
         copies["l", n].wait_send()
         copies["o", n].wait_send()
-    for n in range(NX, NXY):
-        copies["p", n].start()
+    copies["p", 2].start()
     for n in others:
         copies["l", n].wait_recv()
         copies["o", n].wait_recv()
@@ -446,25 +447,34 @@
         mine[:, cols] = residual[:, cols].astype(F32) + jnp.dot(
             ours, wo[:, cols], preferred_element_type=F32
         )
+    for n in range(1, NX):
+        copies["p", n].wait_recv()
+    own_lanes = pl.ds(pl.multiple_of(y * HEAD, HEAD), HEAD)
+    other_lanes = pl.ds(pl.multiple_of((1 - y) * HEAD, HEAD), HEAD)
+
+    def chosen_page(to_y, j):
+        at = table[1, (x * NY + to_y) * SLOTS + j]
+        here = jnp.full((2, PAGE, HEAD), at, jnp.int32) >= 0
+        return jnp.where(here, fetched[jnp.maximum(at, 0), to_y, j].astype(F32), 0.0).astype(BF16)
+
+    for j in range(SLOTS):
+        swapped[j] = chosen_page(1 - y, j)
+    copies["w", 0].start()
+    for j in range(SLOTS):
+        cache_ref[j, :, :, own_lanes] = chosen_page(y, j)
     for n in range(CHUNKS):
         cols = slice(n * CHUNK, (n + 1) * CHUNK)
         copies["t", n].wait_recv()
         out_ref[:, cols] = (mine[:, cols] + incoming[n].astype(F32)).astype(BF16)
-    for n in others:
-        copies["p", n].wait_recv()
+    copies["w", 0].wait_recv()
     for j in range(SLOTS):
-        at = table[1, (x * NY + y) * SLOTS + j]
-        here = jnp.full((2, PAGE, HEAD), at, jnp.int32) >= 0
-        source = jnp.maximum(at, 0)
-        for g in range(NY):
-            page = fetched[source, g, j].astype(F32)
-            cache_ref[j, :, :, g * HEAD : (g + 1) * HEAD] = jnp.where(here, page, 0.0).astype(BF16)
+        cache_ref[j, :, :, other_lanes] = swapping[j]
     for name, copy in copies.items():
         if name[0] not in ("l", "o"):
             copy.wait_send()
 
 
-COPIES = 15 + 16 + 4 * (NXY - 1) + CHUNKS
+COPIES = 15 + 16 + 3 * (NXY - 1) + NX - 1 + CHUNKS + 1
 
 
 def on_device(
@@ -499,6 +509,8 @@
             pltpu.VMEM((NX, NY, 8, 2 * ROWS), F32),
             pltpu.VMEM((NXY, SLOTS, 2, PAGE, HEAD), BF16),
             pltpu.VMEM((NX, NY, SLOTS, 2, PAGE, HEAD), BF16),
+            pltpu.VMEM((SLOTS, 2, PAGE, HEAD), BF16),
+            pltpu.VMEM((SLOTS, 2, PAGE, HEAD), BF16),
             pltpu.VMEM((2, BLOCK, QCOLS), BF16),
             pltpu.VMEM((BLOCK, WIDTH), F32),
             pltpu.VMEM((CHUNKS, BLOCK, CHUNK), BF16),
@@ -508,7 +520,7 @@
             pltpu.SemaphoreType.DMA((COPIES,)),
         ],
         compiler_params=pltpu.CompilerParams(
-            collective_id=1, has_side_effects=True, vmem_limit_bytes=60 * MIB
+            collective_id=1, has_side_effects=True, vmem_limit_bytes=54 * MIB
         ),
         name="layer",
     )(

time: 78.5 us -> 73.7 us (0.939)
  Pallas kernels: 74.3 us -> 69.3 us
    pallas_call x1, Pallas kernels: 72.8 us -> 67.8 us  [on_device(): pl.pallas_call(layer_kernel, out_shape=(jax.ShapeDtypeStruct((BLOCK, WIDT...]
where the time goes in v3:
time: 73.7 us; the launch traced here: 73.3 us
  Pallas kernels  69.3 us (94%)
  local copies, waits for them, and re-layouts  3.34 us (5%)
    pallas_call x1, Pallas kernels, on_device(): pl.pallas_call(layer_kernel, out_shape=(jax.ShapeDtypeStruct((BLOCK, WIDT...  67.8 us
    unnamed x2, local copies, waits for them, and re-layouts  3.34 us
    pallas_call x1, Pallas kernels, make_table(): pl.pallas_call(table_kernel, out_shape=jax.ShapeDtypeStruct((8, HEAD), jn...  1.52 us

profile of v3, /device:TPU:1, one launch (start us, length us, event | category | flops | bytes accessed | tf_op | source)
XLA Modules:
  0.0 73.3 jit_solution(8015140873337374281)
XLA Ops:
  0.6 1.5 %table.1 = s32[8,128]{1,0:T(8,128)} custom-call(s32[1,128]{1,0:T(1,128)} %bitcast.5, s32[4,128]{1,0:T(4,128)} %bitcast.4), custom_call_target="tpu_custom_call" | custom-call | tf_op jit(solution)/shard_map/table/pallas_call | solution.py:165
  2.2 67.8 %layer.1 = (bf16[64,2048]{1,0:T(8,128)(2,1)}, bf16[8,2,32,256]{3,2,1,0:T(8,128)(2,1)}) custom-call(s32[4]{0:T(128)} %lengths.1, s32[128]{0:T(128)} %split.1, s32[8,128]{1,0:T(8,128)} %table.1, bf16[128,2048]{1,0:T(8,128)(2,1)} %tok_hbm.1, f32[1,2048]{1,0:T(1,128)} %bitcast.3, bf16[2048,512]{1,0:T(8,128)(2,1)} %wq_hbm.1, bf16[2048,256]{1,0:T(8,128)(2,1)} %wk_hbm.1, ...), custom_call_target="tpu_custom_call" | custom-call | tf_op jit(solution)/shard_map/layer/pallas_call | solution.py:483
  70.0 1.7 %copy.14 = bf16[64,2048]{1,0:T(8,128)(2,1)} copy(bf16[64,2048]{1,0:T(8,128)(2,1)} %get-tuple-element.4) | data formatting | bytes 524288
  71.6 1.7 %copy.15 = bf16[8,2,32,256]{3,2,1,0:T(8,128)(2,1)} copy(bf16[8,2,32,256]{3,2,1,0:T(8,128)(2,1)} %get-tuple-element.5) | data formatting | bytes 524288

commit v4 on v3

--- a/solution.py
+++ b/solution.py
@@ -61,21 +61,6 @@
         for j in range(NY)
         for i in range(NX)
     ]
-
-
-NODES = [(0, 0)]
-for _k in (1, 2, 3):
-    NODES += [(1, -_k), (1, _k), (0, -_k), (0, _k)]
-NODES += [(1, 4), (0, 4)]
-
-
-def passed_on(own, dz):
-    out = []
-    if -3 < dz <= 0 or (dz == -3 and own):
-        out.append(("up", dz - 1))
-    if 0 <= dz < 3 or (dz == 3 and not own):
-        out.append(("down", dz + 1))
-    return [(to, 4 if abs(to_dz) == 4 else to_dz) for to, to_dz in out]
 
 
 def prompt_start(pos, begins):
@@ -320,7 +305,7 @@
                 ]
             return 0
 
-        lax.fori_loop(0, NXY * SLOTS, one, 0)
+        lax.fori_loop(0, NXY * SLOTS, one, 0, unroll=8)
 
     def sibling(*places):
         for own, dz in places:
@@ -365,9 +350,6 @@
         @pl.when(i == 7)
         def _():
             sibling((1, 4), (0, 4))
-            build_pages()
-            copies["p", 1].start()
-            copies["p", 3].start()
 
         half = (i + 1) // 2
         far = (z + NZ + half * (1 - i % 2 * 2)) % NZ
@@ -410,6 +392,9 @@
     for n in others:
         copies["l", n].start()
         copies["o", n].start()
+    build_pages()
+    for n in range(1, NX):
+        copies["p", n].start()
     held[x, y] = parts[x * NY + y]
     lses[x, y] = levels[x * NY + y]
     fetched[x] = pages[pl.ds(x * NY, NY)]
@@ -417,7 +402,6 @@
     for n in others:
         copies["l", n].wait_send()
         copies["o", n].wait_send()
-    copies["p", 2].start()
     for n in others:
         copies["l", n].wait_recv()
         copies["o", n].wait_recv()

time: 73.7 us -> 68.3 us (0.927)
  the two profiles are of different devices: /device:TPU:1 before, /device:TPU:8 now
where the time goes in v4:
time: 68.3 us; the launch traced here: 68.1 us
  Pallas kernels  64.2 us (94%)
  local copies, waits for them, and re-layouts  3.34 us (5%)
    pallas_call x1, Pallas kernels, on_device(): pl.pallas_call(layer_kernel, out_shape=(jax.ShapeDtypeStruct((BLOCK, WIDT...  62.6 us
    unnamed x2, local copies, waits for them, and re-layouts  3.34 us
    pallas_call x1, Pallas kernels, make_table(): pl.pallas_call(table_kernel, out_shape=jax.ShapeDtypeStruct((8, HEAD), jn...  1.52 us

profile of v4, /device:TPU:8, one launch (start us, length us, event | category | flops | bytes accessed | tf_op | source)
XLA Modules:
  0.0 68.1 jit_solution(13951788732808160567)
XLA Ops:
  0.6 1.5 %table.1 = s32[8,128]{1,0:T(8,128)} custom-call(s32[1,128]{1,0:T(1,128)} %bitcast.5, s32[4,128]{1,0:T(4,128)} %bitcast.4), custom_call_target="tpu_custom_call" | custom-call | tf_op jit(solution)/shard_map/table/pallas_call | solution.py:150
  2.2 62.6 %layer.1 = (bf16[64,2048]{1,0:T(8,128)(2,1)}, bf16[8,2,32,256]{3,2,1,0:T(8,128)(2,1)}) custom-call(s32[4]{0:T(128)} %lengths.1, s32[128]{0:T(128)} %split.1, s32[8,128]{1,0:T(8,128)} %table.1, bf16[128,2048]{1,0:T(8,128)(2,1)} %tok_hbm.1, f32[1,2048]{1,0:T(1,128)} %bitcast.3, bf16[2048,512]{1,0:T(8,128)(2,1)} %wq_hbm.1, bf16[2048,256]{1,0:T(8,128)(2,1)} %wk_hbm.1, ...), custom_call_target="tpu_custom_call" | custom-call | tf_op jit(solution)/shard_map/layer/pallas_call | solution.py:467
  64.8 1.7 %copy.14 = bf16[64,2048]{1,0:T(8,128)(2,1)} copy(bf16[64,2048]{1,0:T(8,128)(2,1)} %get-tuple-element.4) | data formatting | bytes 524288
  66.5 1.7 %copy.15 = bf16[8,2,32,256]{3,2,1,0:T(8,128)(2,1)} copy(bf16[8,2,32,256]{3,2,1,0:T(8,128)(2,1)} %get-tuple-element.5) | data formatting | bytes 524288

commit v5 on v4

--- a/solution.py
+++ b/solution.py
@@ -114,46 +114,38 @@
     return jnp.sum(jnp.where(eye, jnp.broadcast_to(row, (HEAD, HEAD)), 0.0), 1, keepdims=True)
 
 
-def table_kernel(split_ref, slot_ref, table_ref):
-    y, x, z, c = coords(lax.axis_index("seq"))
+def make_table(table_ref, split_ref, slot_ref, y, x, z, c):
     eye = diagonal()
     sub = lax.broadcasted_iota(jnp.int32, (HEAD, HEAD), 0)
     row_lane = lax.broadcasted_iota(jnp.int32, (1, HEAD), 1)
 
     def pick(mask, value):
-        return jnp.sum(jnp.where(mask, value, 0.0), 0, keepdims=True)
+        return jnp.sum(jnp.where(mask, value, 0), 0, keepdims=True)
+
+    def upright(row):
+        return jnp.broadcast_to(
+            jnp.sum(jnp.where(eye, jnp.broadcast_to(row, (HEAD, HEAD)), 0), 1, keepdims=True), (HEAD, HEAD)
+        )
 
     ys, xs, zs, cs = coords(sub)
-    split_col = jnp.broadcast_to(stand(split_ref[...].astype(F32), eye), (HEAD, HEAD))
+    split_col = upright(split_ref[...])
     halves = (split_col, 2 * NSEQ - 1 - split_col)
     place = row_lane // SLOTS % NXY
     wanted = index_of(place % NY, place // NY, z, c) * SLOTS + row_lane % SLOTS
-    page, found = 0.0, 0.0
+    page, found = 0, 0
     for k in range(4):
-        slots = jnp.broadcast_to(stand(slot_ref[k : k + 1, :].astype(F32), eye), (HEAD, HEAD))
-        hit = slots == wanted.astype(F32)
-        page += pick(hit, (sub + HEAD * k).astype(F32))
-        found += pick(hit, 1.0)
-    page = page.astype(jnp.int32)
-    block = (page // 2).astype(F32)
-    at, column = 0.0, 0.0
+        hit = upright(slot_ref[k : k + 1, :]) == wanted
+        page += pick(hit, sub + HEAD * k)
+        found += pick(hit, 1)
+    block = page // 2
+    at, column = 0, 0
     for h in range(2):
         hit = halves[h] == block
-        at += pick(hit & (xs == x), (2 * ((zs * NC + cs) * NY + ys) + h).astype(F32))
-        column += pick(hit, xs.astype(F32))
-    table_ref[0:1, :] = at.astype(jnp.int32) * 2 + page % 2
-    table_ref[1:2, :] = jnp.where(found > 0.5, column, -1.0).astype(jnp.int32)
+        at += pick(hit & (xs == x), 2 * ((zs * NC + cs) * NY + ys) + h)
+        column += pick(hit, xs)
+    table_ref[0:1, :] = jnp.minimum(at * 2 + page % 2, 2 * NSEQ // 2 - 1)
+    table_ref[1:2, :] = jnp.where(found > 0, jnp.minimum(column, NX - 1), -1)
     table_ref[2:, :] = jnp.zeros((6, HEAD), jnp.int32)
-
-
-def make_table(block_split, page_slot):
-    return pl.pallas_call(
-        table_kernel,
-        out_shape=jax.ShapeDtypeStruct((8, HEAD), jnp.int32),
-        in_specs=[VMEM, VMEM],
-        out_specs=VMEM,
-        name="table",
-    )(block_split.reshape(1, NSEQ), page_slot.reshape(4, HEAD))
 
 
 NODES = [(0, 0)]
@@ -173,9 +165,9 @@
 
 
 def layer_kernel(
-    lengths, split, table, tok_hbm, gain_ref, wq_hbm, wk_hbm, wv_hbm, wo_hbm, freq_ref,
+    lengths, split, tok_hbm, gain_ref, wq_hbm, wk_hbm, wv_hbm, wo_hbm, freq_ref, split_ref, slot_ref,
     out_ref, cache_ref,
-    tok, wq, wk, wv, wo, normed, proj, kv, q, kvall, qall, turned, acc, top,
+    tok, wq, wk, wv, wo, normed, proj, kv, q, kvall, qall, turned, acc, top, table_v, table,
     parts, levels, held, lses, pages, fetched, swapped, swapping, context, mine, outgoing, incoming,
     load_sem, send_sem, recv_sem,
 ):
@@ -280,6 +272,9 @@
     for n in others:
         copies["q", n].start()
 
+    make_table(table_v, split_ref, slot_ref, y, x, z, c)
+    to_scalars = pltpu.make_async_copy(table_v, table, load_sem.at[14])
+    to_scalars.start()
     lane = lax.broadcasted_iota(jnp.int32, (1, ROWS), 1)
     pos = []
     for px in range(NX):
@@ -295,6 +290,7 @@
     top[...] = jnp.full_like(top, FLOOR)
     acc[...] = jnp.zeros_like(acc)
     inner = lax.broadcasted_iota(jnp.int32, (BLOCK, LANES), 0)
+    to_scalars.wait()
 
     def build_pages():
         def one(n, _):
@@ -383,15 +379,16 @@
     total = acc[HEAD : HEAD + 1, :]
     seen = total > 0.0
     safe = jnp.where(seen, total, 1.0)
-    lse = jnp.where(seen, top[...] * SCALE2 + jnp.log2(safe), FAR)
-    inverse = 1.0 / safe
-    for n in range(NXY):
-        cols = slice(n * 2 * ROWS, (n + 1) * 2 * ROWS)
-        parts[n] = (acc[:HEAD, cols] * inverse[:, cols]).astype(BF16)
-        levels[n] = jnp.broadcast_to(lse[:, cols], (8, 2 * ROWS))
-    for n in others:
-        copies["l", n].start()
-        copies["o", n].start()
+    top[...] = jnp.where(seen, top[...] * SCALE2 + jnp.log2(safe), FAR)
+    acc[HEAD : HEAD + 1, :] = 1.0 / safe
+    for n in list(others) + [0]:
+        to = peers[n][0] * NY + peers[n][1]
+        cols = pl.ds(pl.multiple_of(to * 2 * ROWS, 2 * ROWS), 2 * ROWS)
+        levels[to] = jnp.broadcast_to(top[:, cols], (8, 2 * ROWS))
+        parts[to] = (acc[:HEAD, cols] * acc[HEAD : HEAD + 1, cols]).astype(BF16)
+        if n:
+            copies["l", n].start()
+            copies["o", n].start()
     build_pages()
     for n in range(1, NX):
         copies["p", n].start()
@@ -470,7 +467,7 @@
             jax.ShapeDtypeStruct((BLOCK, WIDTH), BF16),
             jax.ShapeDtypeStruct((SLOTS, 2, PAGE, KCOLS), BF16),
         ),
-        in_specs=[SMEM, SMEM, SMEM, HBM, VMEM, HBM, HBM, HBM, HBM, VMEM],
+        in_specs=[SMEM, SMEM, HBM, VMEM, HBM, HBM, HBM, HBM, VMEM, VMEM, VMEM],
         out_specs=(VMEM, VMEM),
         scratch_shapes=[
             pltpu.VMEM((ROWS, WIDTH), BF16),
@@ -487,6 +484,8 @@
             pltpu.VMEM((HEAD + EXTRA, KEYS), BF16),
             pltpu.VMEM((HEAD + EXTRA, LANES), F32),
             pltpu.VMEM((1, LANES), F32),
+            pltpu.VMEM((8, HEAD), jnp.int32),
+            pltpu.SMEM((8, HEAD), jnp.int32),
             pltpu.VMEM((NXY, HEAD, 2 * ROWS), BF16),
             pltpu.VMEM((NXY, 8, 2 * ROWS), F32),
             pltpu.VMEM((NX, NY, HEAD, 2 * ROWS), BF16),
@@ -499,7 +498,7 @@
             pltpu.VMEM((BLOCK, WIDTH), F32),
             pltpu.VMEM((CHUNKS, BLOCK, CHUNK), BF16),
             pltpu.VMEM((CHUNKS, BLOCK, CHUNK), BF16),
-            pltpu.SemaphoreType.DMA((14,)),
+            pltpu.SemaphoreType.DMA((15,)),
             pltpu.SemaphoreType.DMA((COPIES,)),
             pltpu.SemaphoreType.DMA((COPIES,)),
         ],
@@ -508,8 +507,8 @@
         ),
         name="layer",
     )(
-        lengths, block_split, make_table(block_split, page_slot), tokens, norm_gain.reshape(1, WIDTH), w_query,
-        key_projection, value_projection, w_out, jnp.asarray(FREQ),
+        lengths, block_split, tokens, norm_gain.reshape(1, WIDTH), w_query, key_projection, value_projection,
+        w_out, jnp.asarray(FREQ), block_split.reshape(1, NSEQ), page_slot.reshape(4, HEAD),
     )
 
 

time: 68.3 us -> 66.9 us (0.980)
  Pallas kernels: 64.2 us -> 62.7 us
    pallas_call x1 -> x0, Pallas kernels: 1.52 us -> none  [make_table(): pl.pallas_call(table_kernel, out_shape=jax.ShapeDtypeStruct((8, HEAD), jn...]
where the time goes in v5:
time: 66.9 us; the launch traced here: 66.7 us
  Pallas kernels  62.7 us (94%)
  local copies, waits for them, and re-layouts  3.34 us (5%)
    pallas_call x1, Pallas kernels, on_device(): pl.pallas_call(layer_kernel, out_shape=(jax.ShapeDtypeStruct((BLOCK, WIDT...  62.7 us
    unnamed x2, local copies, waits for them, and re-layouts  3.34 us

profile of v5, /device:TPU:8, one launch (start us, length us, event | category | flops | bytes accessed | tf_op | source)
XLA Modules:
  0.0 66.7 jit_solution(13130815157333862953)
XLA Ops:
  0.6 62.7 %layer.1 = (bf16[64,2048]{1,0:T(8,128)(2,1)}, bf16[8,2,32,256]{3,2,1,0:T(8,128)(2,1)}) custom-call(s32[4]{0:T(128)} %lengths.1, s32[128]{0:T(128)} %split.1, bf16[128,2048]{1,0:T(8,128)(2,1)} %tok_hbm.1, f32[1,2048]{1,0:T(1,128)} %bitcast.3, bf16[2048,512]{1,0:T(8,128)(2,1)} %wq_hbm.1, bf16[2048,256]{1,0:T(8,128)(2,1)} %wk_hbm.1, bf16[2048,256]{1,0:T(8,128)(2,1)} %wv_hbm.1, ...), custom_call_target="tpu_custom_call" | custom-call | tf_op jit(solution)/shard_map/layer/pallas_call | solution.py:464
  63.4 1.7 %copy.14 = bf16[64,2048]{1,0:T(8,128)(2,1)} copy(bf16[64,2048]{1,0:T(8,128)(2,1)} %get-tuple-element.4) | data formatting | bytes 524288
  65.0 1.7 %copy.15 = bf16[8,2,32,256]{3,2,1,0:T(8,128)(2,1)} copy(bf16[8,2,32,256]{3,2,1,0:T(8,128)(2,1)} %get-tuple-element.5) | data formatting | bytes 524288
